TPU v7x, 256 devices: a whole 4x4x8 slice. The times are simulated.
256 devices in a mesh: layer: 4 (over y), front: 64 (over z, x, core).
Axes of the slice: x: 4, y: 4, z: 8, core: 2. Of those that a mesh axis runs over, the one named last changes fastest.
Arguments:
- right_sides: float32 [4, 2, 4, 8192], P('layer', None, None, 'front'), may hold values from -6 to 6
- leaf_inverse: bfloat16 [4, 2, 8192, 128], P('layer', None, 'front'), may hold values from -0.375 to 0.375
- couple_above: bfloat16 [4, 2, 8192, 128], P('layer', None, 'front'), may hold values from -0.1875 to 0.1875
- couple_below: bfloat16 [4, 2, 8192, 128], P('layer', None, 'front'), may hold values from -0.1875 to 0.1875
- sep_gather: bfloat16 [4, 2, 5120, 8192], P('layer', None, None, 'front'), may hold values from -0.046875 to 0.046875
- sep_inverse: bfloat16 [4, 2, 5120, 5120], P('layer', None, 'front'), may hold values from -0.0625 to 0.0625
- sep_spread: bfloat16 [4, 2, 8192, 5120], P('layer', None, 'front'), may hold values from -0.0625 to 0.0625
- panel_owner: int32 [4, 64], P('layer'), may hold values from 0 to 63, each once within a row
Outputs:
- solution: float32 [4, 2, 4, 8192], P('layer', None, None, 'front')
Inputs may be any that keep to these rules, and one draw needn't show every extreme that they name: Each row of panel_owner names every slot 0 to 63 once.
All inputs are finite; a program needn't handle non-finite values.
Results may differ from a plain program's by a relative error of at most 0.023.
Values may be sent and summed in bfloat16 or wider, within the bound.
A program may use at most 128 MiB of HBM per device.

v0:
```python
import jax
import jax.numpy as jnp
from jax import lax
from jax.sharding import PartitionSpec as P


def from_behind(block, axis, distance):
    devices = range(lax.axis_size(axis))
    route = [(i - distance, i) for i in devices if i - distance in devices]
    return lax.ppermute(block, axis, route)


def dense_apply(matrix, vector):

    def single(left, right):
        return jnp.dot(right, left.T, preferred_element_type=jnp.float32)

    real_part = single(matrix[0], vector[0]) - single(matrix[1], vector[1])
    imag_part = single(matrix[0], vector[1]) + single(matrix[1], vector[0])
    return jnp.stack([real_part, imag_part])


def layer_solve(source, leaf, gather_map, sep_panel, spread, owner_row):
    leaf_values = dense_apply(leaf, source.astype(jnp.bfloat16))
    partial_sums = dense_apply(gather_map, leaf_values.astype(jnp.bfloat16))
    sep_rounded = lax.psum(partial_sums, "front").astype(jnp.bfloat16)
    own_rows = dense_apply(sep_panel, sep_rounded).astype(jnp.bfloat16)
    stored = lax.all_gather(own_rows, "front", axis=2, tiled=True)
    count = stored.shape[1]
    panels = stored.reshape(2, count, owner_row.shape[0], own_rows.shape[2])
    sep_values = jnp.take(panels, owner_row, axis=2).reshape(2, count, stored.shape[2])
    return leaf_values - dense_apply(spread, sep_values)


def local(
    right_sides,
    leaf_inverse,
    couple_above,
    couple_below,
    sep_gather,
    sep_inverse,
    sep_spread,
    panel_owner,
):
    depth = lax.axis_size("layer")
    owner_row = panel_owner[0]
    sources = right_sides[0]

    def solve(source):
        return layer_solve(
            source, leaf_inverse[0], sep_gather[0], sep_inverse[0], sep_spread[0], owner_row
        )

    forward = solve(sources)
    for step_index in range(depth - 1):
        from_prev = from_behind(forward.astype(jnp.bfloat16), "layer", 1)
        forward = solve(sources - dense_apply(couple_above[0], from_prev))
    solution = forward
    for step_index in range(depth - 1):
        from_next = from_behind(solution.astype(jnp.bfloat16), "layer", -1)
        solution = forward - solve(dense_apply(couple_below[0], from_next))
    return solution[None]


def solution(mesh):
    return jax.shard_map(
        local,
        mesh=mesh,
        in_specs=(
            P("layer", None, None, "front"),
            P("layer", None, "front", None),
            P("layer", None, "front", None),
            P("layer", None, "front", None),
            P("layer", None, None, "front"),
            P("layer", None, "front", None),
            P("layer", None, "front", None),
            P("layer", None),
        ),
        out_specs=P("layer", None, None, "front"),
        check_vma=False,
    )
```

profile of v0, /device:TPU:1, one launch (start us, length us, event | category | flops | bytes accessed | tf_op | source)
XLA Modules:
  0.0 2287.0 jit_solution(15067838010511855414)
XLA Ops:
  10.3 249.5 %all-reduce.7 = bf16[2,4,5120]{2,1,0:T(4,128)(2,1)S(1)} all-reduce(f32[2,4,5120]{2,1,0:T(4,128)S(1)} %pad_maximum_fusion), channel_id=1, replica_groups=mesh['layer'=4,'front'=64] {'front'}, use_global_device_ids=true, to_apply=%region_0.0 | all-reduce | flops 40960 | bytes 245760 | tf_op jit(solution)/shard_map/psum | solution.py:26
  263.7 58.7 %all_gather.21 = bf16[2,4,5120]{1,0,2:T(2,128)(2,1)} all-gather(bf16[2,4,80]{1,0,2:T(2,128)(2,1)S(1)} %copy.58), channel_id=1, replica_groups=mesh['layer'=4,'front'=64] {'front'}, dimensions={2}, use_global_device_ids=true | all-gather | bytes 83200 | tf_op jit(solution)/shard_map/all_gather | solution.py:28
  322.4 5.4 copy.60
  333.7 3.2 collective-permute-start
  340.8 243.3 %all-reduce.8 = bf16[2,4,5120]{2,1,0:T(4,128)(2,1)S(1)} all-reduce(f32[2,4,5120]{2,1,0:T(4,128)S(1)} %pad_maximum_fusion.1), channel_id=1, replica_groups=mesh['layer'=4,'front'=64] {'front'}, use_global_device_ids=true, to_apply=%region_1.0 | all-reduce | flops 40960 | bytes 245760 | tf_op jit(solution)/shard_map/psum | solution.py:26
  587.9 59.3 %all_gather.22 = bf16[2,4,5120]{1,0,2:T(2,128)(2,1)} all-gather(bf16[2,4,80]{1,0,2:T(2,128)(2,1)S(1)} %copy.63), channel_id=1, replica_groups=mesh['layer'=4,'front'=64] {'front'}, dimensions={2}, use_global_device_ids=true | all-gather | bytes 83200 | tf_op jit(solution)/shard_map/all_gather | solution.py:28
  647.2 5.4 copy.65
  655.7 1.9 fusion.34
  659.8 3.6 collective-permute-start.1
  667.2 243.3 %all-reduce.9 = bf16[2,4,5120]{2,1,0:T(4,128)(2,1)S(1)} all-reduce(f32[2,4,5120]{2,1,0:T(4,128)S(1)} %pad_maximum_fusion.2), channel_id=1, replica_groups=mesh['layer'=4,'front'=64] {'front'}, use_global_device_ids=true, to_apply=%region_2.4 | all-reduce | flops 40960 | bytes 245760 | tf_op jit(solution)/shard_map/psum | solution.py:26
  914.4 58.7 %all_gather.23 = bf16[2,4,5120]{1,0,2:T(2,128)(2,1)} all-gather(bf16[2,4,80]{1,0,2:T(2,128)(2,1)S(1)} %copy.68), channel_id=1, replica_groups=mesh['layer'=4,'front'=64] {'front'}, dimensions={2}, use_global_device_ids=true | all-gather | bytes 83200 | tf_op jit(solution)/shard_map/all_gather | solution.py:28
  973.1 5.4 copy.70
  981.6 1.9 fusion.30
  985.7 3.6 collective-permute-start.2
  993.1 243.5 %all-reduce.10 = bf16[2,4,5120]{2,1,0:T(4,128)(2,1)S(1)} all-reduce(f32[2,4,5120]{2,1,0:T(4,128)S(1)} %pad_maximum_fusion.3), channel_id=1, replica_groups=mesh['layer'=4,'front'=64] {'front'}, use_global_device_ids=true, to_apply=%region_3.5 | all-reduce | flops 40960 | bytes 245760 | tf_op jit(solution)/shard_map/psum | solution.py:26
  1240.5 58.7 %all_gather.24 = bf16[2,4,5120]{1,0,2:T(2,128)(2,1)} all-gather(bf16[2,4,80]{1,0,2:T(2,128)(2,1)S(1)} %copy.73), channel_id=1, replica_groups=mesh['layer'=4,'front'=64] {'front'}, dimensions={2}, use_global_device_ids=true | all-gather | bytes 83200 | tf_op jit(solution)/shard_map/all_gather | solution.py:28
  1299.2 5.4 copy.75
  1307.7 1.9 fusion.26
  1313.2 3.3 collective-permute-done.3
  1319.5 243.3 %all-reduce.11 = bf16[2,4,5120]{2,1,0:T(4,128)(2,1)S(1)} all-reduce(f32[2,4,5120]{2,1,0:T(4,128)S(1)} %pad_maximum_fusion.4), channel_id=1, replica_groups=mesh['layer'=4,'front'=64] {'front'}, use_global_device_ids=true, to_apply=%region_4.6 | all-reduce | flops 40960 | bytes 245760 | tf_op jit(solution)/shard_map/psum | solution.py:26
  1566.7 58.7 %all_gather.25 = bf16[2,4,5120]{1,0,2:T(2,128)(2,1)} all-gather(bf16[2,4,80]{1,0,2:T(2,128)(2,1)S(1)} %copy.78), channel_id=1, replica_groups=mesh['layer'=4,'front'=64] {'front'}, dimensions={2}, use_global_device_ids=true | all-gather | bytes 83200 | tf_op jit(solution)/shard_map/all_gather | solution.py:28
  1625.4 5.4 copy.80
  1633.9 1.9 fusion.22
  1639.5 2.8 collective-permute-done.4
  1645.4 243.3 %all-reduce.12 = bf16[2,4,5120]{2,1,0:T(4,128)(2,1)S(1)} all-reduce(f32[2,4,5120]{2,1,0:T(4,128)S(1)} %pad_maximum_fusion.5), channel_id=1, replica_groups=mesh['layer'=4,'front'=64] {'front'}, use_global_device_ids=true, to_apply=%region_5.7 | all-reduce | flops 40960 | bytes 245760 | tf_op jit(solution)/shard_map/psum | solution.py:26
  1892.6 58.7 %all_gather.26 = bf16[2,4,5120]{1,0,2:T(2,128)(2,1)} all-gather(bf16[2,4,80]{1,0,2:T(2,128)(2,1)S(1)} %copy.83), channel_id=1, replica_groups=mesh['layer'=4,'front'=64] {'front'}, dimensions={2}, use_global_device_ids=true | all-gather | bytes 83200 | tf_op jit(solution)/shard_map/all_gather | solution.py:28
  1951.3 5.4 copy.85
  1959.8 1.9 fusion.18
  1965.3 3.0 collective-permute-done.5
  1971.3 243.4 %all-reduce.13 = bf16[2,4,5120]{2,1,0:T(4,128)(2,1)S(1)} all-reduce(f32[2,4,5120]{2,1,0:T(4,128)S(1)} %pad_maximum_fusion.6), channel_id=1, replica_groups=mesh['layer'=4,'front'=64] {'front'}, use_global_device_ids=true, to_apply=%region_6.8 | all-reduce | flops 40960 | bytes 245760 | tf_op jit(solution)/shard_map/psum | solution.py:26
  2218.5 59.0 %all_gather.27 = bf16[2,4,5120]{1,0,2:T(2,128)(2,1)} all-gather(bf16[2,4,80]{1,0,2:T(2,128)(2,1)S(1)} %copy.88), channel_id=1, replica_groups=mesh['layer'=4,'front'=64] {'front'}, dimensions={2}, use_global_device_ids=true | all-gather | bytes 83200 | tf_op jit(solution)/shard_map/all_gather | solution.py:28
  2277.5 5.5 copy.90
  (265 shorter events, 97.6 us)
Async XLA Ops:
  0.0 9.3 copy-start
  259.8 3.1 copy-start.12
  329.1 3.7 copy-start.1
  332.8 4.9 copy-start.9
  332.8 5.4 copy-start.11
  332.8 5.5 copy-start.8
  333.7 3.9 collective-permute-start
  584.1 3.1 copy-start.13
  655.6 3.7 copy-start.2
  659.8 4.3 collective-permute-start.1
  910.5 3.1 copy-start.14
  981.6 3.7 copy-start.3
  985.7 4.3 collective-permute-start.2
  1236.6 3.1 copy-start.15
  1307.7 3.7 copy-start.4
  1309.6 6.9 copy-start.10
  1311.9 4.6 collective-permute-start.3
  1562.8 3.1 copy-start.16
  1633.9 3.7 copy-start.5
  1638.0 4.3 collective-permute-start.4
  1888.7 3.1 copy-start.17
  1959.8 3.7 copy-start.6
  1964.0 4.3 collective-permute-start.5
  1971.3 246.4 %copy-start.18 = (bf16[1,2,80,5120]{3,2,1,0:T(8,128)(2,1)S(1)}, bf16[1,2,80,5120]{3,2,1,0:T(8,128)(2,1)}, u32[]{:S(2)}) copy-start(bf16[1,2,80,5120]{3,2,1,0:T(8,128)(2,1)} %param.15) | copy-start | bytes 4915204
  2277.5 6.7 copy-start.7
where the time goes:
time: 2300 us; the launch traced here: 2290 us
  blocking collectives  2120 us (92%)
  matrix products  87.5 us (4%)
  local copies, waits for them, and re-layouts  46.6 us (2%)
    psum x7, blocking collectives, layer_solve(): sep_rounded = lax.psum(partial_sums, 'front').astype(jnp.bfloat16)  1710 us
    all_gather x7, blocking collectives, layer_solve(): stored = lax.all_gather(own_rows, 'front', axis=2, tiled=True)  412 us
    dot_general x136, matrix products, single(): return jnp.dot(right, left.T, preferred_element_type=jnp.float32)  87.5 us
  transfers between devices with their start and end apart: 6, of which 6 were waited for; matrix products, arithmetic and copies ran while one was open for 0% of the time, Pallas kernels for 0%

commit v1 on v0

v1 whole, which is shorter than its diff:
```python
import functools

import jax
import jax.numpy as jnp
from jax import lax
from jax.experimental import pallas as pl
from jax.experimental.pallas import tpu as pltpu
from jax.sharding import PartitionSpec as P

MESH = pl.DeviceIdType.MESH
F32 = jnp.float32
BF16 = jnp.bfloat16
ROWS = 8
GROUP = 8


def widen(v):
    turned = pltpu.roll(v, 4, 0)
    row = lax.broadcasted_iota(jnp.int32, v.shape, 0)
    turned = jnp.where(row < 4, -turned, turned)
    return jnp.concatenate([v, turned], axis=1).astype(BF16)


def times(wide, matrix):
    return lax.dot_general(wide, matrix, (((1,), (1,)), ((), ())), preferred_element_type=F32)


def kernel(
    depth, cells, sep, panel,
    owner, rs, leaf_h, above_h, below_h, gather_h, inv_h, spread_h,
    out,
    leaf, above, below, gath, qmat, spread,
    abuf, arecv, bbuf, brecv, cbuf, crecv, dbuf, vall, natural, fbuf, frecv, held,
    load_sem, q_send, q_recv, send_sem, recv_sem, f_send, f_recv,
):
    ly = lax.axis_index("layer")
    me = lax.axis_index("front")
    z, r = me // GROUP, lax.rem(me, GROUP)
    block = sep // GROUP

    def row_peer(k):
        return (ly, z * GROUP + lax.rem(r + k, GROUP))

    def col_peer(k):
        return (ly, lax.rem(z + k, GROUP) * GROUP + r)

    def load(src, dst, at):
        copy = pltpu.make_async_copy(src, dst, load_sem.at[at])
        copy.start()
        return copy

    loads = []
    n = 0
    for src, dst, width in (
        (leaf_h, leaf, cells), (gather_h, gath, cells), (spread_h, spread, sep),
        (above_h, above, cells), (below_h, below, cells),
    ):
        pair = []
        for part in range(2):
            pair.append(load(src.at[part], dst.at[:, pl.ds(part * width, width)], n))
            n += 1
        loads.append(pair)
    own_q = []
    for part in range(2):
        own_q.append(load(
            inv_h.at[part, :, pl.ds(pl.multiple_of(r * block, 128), block)],
            qmat.at[r, pl.ds(0, panel), pl.ds(part * block, block)], n))
        n += 1

    barrier = pltpu.get_barrier_semaphore()
    for k in range(1, GROUP):
        pl.semaphore_signal(barrier, inc=1, device_id=row_peer(k), device_id_type=MESH)
        pl.semaphore_signal(barrier, inc=1, device_id=col_peer(k), device_id_type=MESH)

    @pl.when(ly > 0)
    def _():
        pl.semaphore_signal(barrier, inc=1, device_id=(ly - 1, me), device_id_type=MESH)

    @pl.when(ly < depth - 1)
    def _():
        pl.semaphore_signal(barrier, inc=1, device_id=(ly + 1, me), device_id_type=MESH)

    ends = (ly == 0).astype(jnp.int32) + (ly == depth - 1).astype(jnp.int32)
    pl.semaphore_wait(barrier, 2 * (GROUP - 1) + 2 - ends)

    q_copies = []
    for k in range(1, GROUP):
        to = lax.rem(r + k, GROUP)
        for part in range(2):
            copy = pltpu.make_async_remote_copy(
                src_ref=inv_h.at[part, :, pl.ds(pl.multiple_of(to * block, 128), block)],
                dst_ref=qmat.at[r, pl.ds(0, panel), pl.ds(part * block, block)],
                send_sem=q_send.at[k - 1, part],
                recv_sem=q_recv.at[k - 1, part],
                device_id=row_peer(k), device_id_type=MESH)
            copy.start()
            q_copies.append(copy)
    qmat[:, panel:, :] = jnp.zeros((GROUP, 128 - panel, 2 * block), BF16)

    order = (4, 3, 5, 2, 6, 1, 7)

    def wait_all(ref, sem):
        pltpu.make_async_copy(ref, ref, sem).wait()

    def exchange(s, phase, peer, src, recv, local):
        copies = []
        for k in order:
            copy = pltpu.make_async_remote_copy(
                src_ref=src(k), dst_ref=recv.at[s, k - 1],
                send_sem=send_sem.at[s, phase], recv_sem=recv_sem.at[s, phase],
                device_id=peer(k), device_id_type=MESH)
            copy.start()
        wait_all(recv.at[s], recv_sem.at[s, phase])
        total = local
        for k in range(GROUP - 1):
            total = total + recv[s, k].astype(F32)
        return total

    def solve(s, source):
        leaf_values = times(widen(source), leaf[...])
        wide = widen(leaf_values)
        for j in range(GROUP):
            abuf[s, j] = times(wide, gath[pl.ds(j * block, block), :]).astype(BF16)
        mine = exchange(s, 0, row_peer, lambda k: abuf.at[s, lax.rem(r + k, GROUP)], arecv, abuf[s, r].astype(F32))
        bbuf[s] = mine.astype(BF16)
        sums = exchange(s, 1, col_peer, lambda k: bbuf.at[s], brecv, mine)
        wide = widen(sums)
        for c in range(GROUP):
            cbuf[s, c] = times(wide, qmat[c]).astype(BF16)
        values = exchange(s, 2, row_peer, lambda k: cbuf.at[s], crecv, cbuf[s].astype(F32))
        dbuf[s] = values.astype(BF16)
        for k in order:
            pltpu.make_async_remote_copy(
                src_ref=dbuf.at[s], dst_ref=vall.at[s, z],
                send_sem=send_sem.at[s, 3], recv_sem=recv_sem.at[s, 3],
                device_id=col_peer(k), device_id_type=MESH).start()
        vall[s, z] = dbuf[s]
        wait_all(vall.at[s, pl.ds(0, GROUP - 1)], recv_sem.at[s, 3])
        lane = lax.broadcasted_iota(jnp.int32, (ROWS, 128), 1)
        tile, at = None, 0
        for p in range(sep // panel):
            slot = owner[p]
            chunk = vall[s, slot // GROUP, lax.rem(slot, GROUP)].astype(F32)
            start = p * panel - at * 128
            moved = pltpu.roll(chunk, start, 1) if start else chunk
            tile = moved if tile is None else jnp.where(lane >= start, moved, tile)
            if start + panel >= 128:
                natural[:, at * 128:(at + 1) * 128] = tile
                at += 1
                tile = moved if start + panel > 128 else None
        wide = widen(natural[...])
        return leaf_values - times(wide, spread[...])

    def hop(s, to, value):
        fbuf[s] = value.astype(BF16)
        return pltpu.make_async_remote_copy(
            src_ref=fbuf.at[s], dst_ref=frecv.at[s], send_sem=f_send.at[s], recv_sem=f_recv.at[s],
            device_id=(to, me), device_id_type=MESH)

    def sent(s):
        for phase, buf in ((0, arecv), (1, brecv), (2, crecv)):
            wait_all(buf.at[s], send_sem.at[s, phase])
        wait_all(vall.at[s, pl.ds(0, GROUP - 1)], send_sem.at[s, 3])

    for pair in loads:
        for copy in pair:
            copy.wait()

    @pl.when(ly == 0)
    def _():
        held[0] = rs[...]

    @pl.when(ly > 0)
    def _():
        wait_all(frecv.at[0], f_recv.at[0])
        held[0] = rs[...] - times(widen(frecv[0].astype(F32)), above[...])

    for copy in own_q:
        copy.wait()
    for copy in q_copies:
        copy.wait_recv()
    forward = solve(0, held[0])
    held[1] = forward

    @pl.when(ly < depth - 1)
    def _():
        hop(0, ly + 1, held[1]).start()

    @pl.when(ly == depth - 1)
    def _():
        out[...] = held[1]

    @pl.when(ly < depth - 1)
    def _():
        wait_all(frecv.at[1], f_recv.at[1])
        solved = held[1] - solve(1, times(widen(frecv[1].astype(F32)), below[...]))
        out[...] = solved
        wait_all(frecv.at[0], f_send.at[0])

    @pl.when(ly > 0)
    def _():
        copy = hop(1, ly - 1, out[...])
        copy.start()
        copy.wait_send()

    for copy in q_copies:
        copy.wait_send()
    sent(0)

    @pl.when(ly < depth - 1)
    def _():
        sent(1)


def local(right_sides, leaf, above, below, gather, inverse, spread, owner):
    depth = lax.axis_size("layer")
    _, _, count, cells = right_sides.shape
    panel, sep = inverse.shape[2], inverse.shape[3]
    block = sep // GROUP
    vmem = pl.BlockSpec(memory_space=pltpu.VMEM)
    hbm = pl.BlockSpec(memory_space=pl.ANY)
    dma = pltpu.SemaphoreType.DMA
    out = pl.pallas_call(
        functools.partial(kernel, depth, cells, sep, panel),
        out_shape=jax.ShapeDtypeStruct((ROWS, cells), F32),
        in_specs=[pl.BlockSpec(memory_space=pltpu.SMEM), vmem] + [hbm] * 6,
        out_specs=vmem,
        scratch_shapes=[
            pltpu.VMEM((cells, 2 * cells), BF16),
            pltpu.VMEM((cells, 2 * cells), BF16),
            pltpu.VMEM((cells, 2 * cells), BF16),
            pltpu.VMEM((sep, 2 * cells), BF16),
            pltpu.VMEM((GROUP, 128, 2 * block), BF16),
            pltpu.VMEM((cells, 2 * sep), BF16),
            pltpu.VMEM((2, GROUP, ROWS, block), BF16),
            pltpu.VMEM((2, GROUP - 1, ROWS, block), BF16),
            pltpu.VMEM((2, ROWS, block), BF16),
            pltpu.VMEM((2, GROUP - 1, ROWS, block), BF16),
            pltpu.VMEM((2, GROUP, ROWS, 128), BF16),
            pltpu.VMEM((2, GROUP - 1, GROUP, ROWS, 128), BF16),
            pltpu.VMEM((2, GROUP, ROWS, 128), BF16),
            pltpu.VMEM((2, GROUP, GROUP, ROWS, 128), BF16),
            pltpu.VMEM((ROWS, sep), F32),
            pltpu.VMEM((2, ROWS, cells), BF16),
            pltpu.VMEM((2, ROWS, cells), BF16),
            pltpu.VMEM((2, ROWS, cells), F32),
            dma((12,)),
            dma((GROUP - 1, 2)),
            dma((GROUP - 1, 2)),
            dma((2, 4)),
            dma((2, 4)),
            dma((2,)),
            dma((2,)),
        ],
        compiler_params=pltpu.CompilerParams(
            collective_id=0, has_side_effects=True, vmem_limit_bytes=40 * 2**20),
        name="sweep",
    )(owner[0], right_sides.reshape(ROWS, cells), leaf[0], above[0], below[0], gather[0], inverse[0], spread[0])
    return out.reshape(1, 2, count, cells)


def solution(mesh):
    return jax.shard_map(
        local,
        mesh=mesh,
        in_specs=(
            P("layer", None, None, "front"),
            P("layer", None, "front", None),
            P("layer", None, "front", None),
            P("layer", None, "front", None),
            P("layer", None, None, "front"),
            P("layer", None, "front", None),
            P("layer", None, "front", None),
            P("layer", None),
        ),
        out_specs=P("layer", None, None, "front"),
        check_vma=False,
    )
```

time: 2300 us -> 206 us (0.09)
  blocking collectives: 2120 us -> 0 us
  Pallas kernels: 0 us -> 196 us
  matrix products: 87.5 us -> 0 us
  local copies, waits for them, and re-layouts: 46.6 us -> 9.36 us
    psum x7 -> x0, blocking collectives: 1710 us -> none  [layer_solve(): sep_rounded = lax.psum(partial_sums, 'front').astype(jnp.bfloat16)]
    all_gather x7 -> x0, blocking collectives: 412 us -> none  [layer_solve(): stored = lax.all_gather(own_rows, 'front', axis=2, tiled=True)]
    pallas_call x0 -> x1, Pallas kernels: none -> 196 us  [local(): pl.pallas_call(functools.partial(kernel, depth, cells, sep, panel), out_s...]
    dot_general x136 -> x0, matrix products: 87.5 us -> none  [single(): return jnp.dot(right, left.T, preferred_element_type=jnp.float32)]
    reshape x7 -> x0, local copies, waits for them, and re-layouts: 37.8 us -> none  [layer_solve(): panels = stored.reshape(2, count, owner_row.shape[0], own_rows.shape[2])]
  transfers between devices with their start and end apart: 6 -> 0, of which waited for: 6 -> 0; matrix products, arithmetic and copies ran while one was open for 0% -> 0% of each run, Pallas kernels for 0% -> 0%
where the time goes in v1:
time: 206 us
  Pallas kernels  196 us (95%)
  local copies, waits for them, and re-layouts  9.36 us (5%)
    pallas_call x1, Pallas kernels, local(): pl.pallas_call(functools.partial(kernel, depth, cells, sep, panel), out_s...  196 us
    unnamed x17, local copies, waits for them, and re-layouts  9.36 us

profile of v1, /device:TPU:1, one launch (start us, length us, event | category | flops | bytes accessed | tf_op | source)
XLA Modules:
  0.0 205.6 jit_solution(5237786447171119575)
XLA Ops:
  0.0 0.0 copy-start
  0.0 1.7 copy-done
  1.7 0.0 copy-start.1
  1.7 1.7 copy-done.1
  3.5 0.0 copy-start.2
  3.5 1.4 copy-done.2
  4.9 0.0 copy-start.3
  4.9 0.8 copy-done.3
  5.8 0.0 copy-start.4
  5.8 0.8 copy-done.4
  6.6 0.0 copy-start.5
  6.6 0.8 copy-done.5
  7.4 0.0 copy-start.6
  7.4 0.7 copy-done.6
  8.1 0.0 copy-start.7
  8.1 0.7 copy-done.7
  8.8 196.2 %sweep.1 = f32[8,128]{1,0:T(8,128)S(1)} custom-call(s32[64]{0:T(128)S(1)} %bitcast.17, f32[8,128]{1,0:T(8,128)S(1)} %bitcast.16, bf16[2,128,128]{2,1,0:T(8,128)(2,1)S(1)} %bitcast.12, bf16[2,128,128]{2,1,0:T(8,128)(2,1)S(1)} %bitcast.13, bf16[2,128,128]{2,1,0:T(8,128)(2,1)S(1)} %bitcast.14, bf16[2,5120,128]{2,1,0:T(8,128)(2,1)S(1)} %bitcast.9, ...), custom_call_target="tpu_custom_call" | custom-call | tf_op jit(solution)/shard_map/sweep/pallas_call | solution.py:223
  205.0 0.6 copy.10
Async XLA Ops:
  0.0 1.7 copy-start
  1.7 1.7 copy-start.1
  3.5 1.4 copy-start.2
  4.9 0.8 copy-start.3
  5.8 0.8 copy-start.4
  6.6 0.8 copy-start.5
  7.4 0.7 copy-start.6
  8.1 0.7 copy-start.7

commit v2 on v0

v2 whole, which is shorter than its diff:
```python
import functools

import jax
import jax.numpy as jnp
from jax import lax
from jax.experimental import pallas as pl
from jax.experimental.pallas import tpu as pltpu
from jax.sharding import PartitionSpec as P

MESH = pl.DeviceIdType.MESH
F32 = jnp.float32
BF16 = jnp.bfloat16
ROWS = 8
GROUP = 8
ORDER = (4, 3, 5, 2, 6, 1, 7)
PLAIN = 2


def widen(v):
    turned = pltpu.roll(v, 4, 0)
    row = lax.broadcasted_iota(jnp.int32, v.shape, 0)
    turned = jnp.where(row < 4, -turned, turned)
    return jnp.concatenate([v, turned], axis=1).astype(BF16)


def dot_nt(a, b):
    return lax.dot_general(a, b, (((1,), (1,)), ((), ())), preferred_element_type=F32)


def dot_nn(a, b):
    return lax.dot_general(a, b, (((1,), (0,)), ((), ())), preferred_element_type=F32)


def expand(stack, n):
    top, low = stack[:n], stack[n:]
    return jnp.concatenate(
        [jnp.concatenate([top, -low], axis=1), jnp.concatenate([low, top], axis=1)], axis=0).astype(BF16)


def kernel(
    depth, cells, sep, panel,
    slots, rs, leaf_h, above_h, below_h, gather_h, inv_h, spread_h,
    out,
    leaf, above, below, gath, qmat, pnat, leaf_t, la_t, lb_t, xa, xb, qt, pt, pts, po,
    abuf, arecv, bbuf, brecv, cbuf, crecv, dbuf, vall, fbuf, fone, obuf, orecv, frecv,
    const, lead, held, prod,
    load_sem, q_send, q_recv, p_send, p_recv, send_sem, recv_sem, one_send, one_recv,
    y_send, y_recv, o_send, o_recv,
):
    ly = lax.axis_index("layer")
    me = lax.axis_index("front")
    z, r = me // GROUP, lax.rem(me, GROUP)
    block = sep // GROUP

    def row_peer(k):
        return (ly, z * GROUP + lax.rem(r + k, GROUP))

    def col_peer(k):
        return (ly, lax.rem(z + k, GROUP) * GROUP + r)

    def wait_all(ref, sem):
        pltpu.make_async_copy(ref, ref, sem).wait()

    loads = {}
    n = 0
    for name, src, dst in (("leaf", leaf_h, leaf), ("gath", gather_h, gath), ("below", below_h, below), ("above", above_h, above)):
        loads[name] = []
        for part in range(2):
            copy = pltpu.make_async_copy(src.at[part], dst.at[:, pl.ds(part * cells, cells)], load_sem.at[n])
            copy.start()
            loads[name].append(copy)
            n += 1
    loads["spread"] = [pltpu.make_async_copy(spread_h, pnat, load_sem.at[n])]
    loads["spread"][0].start()
    n += 1
    loads["own"] = []
    for part in range(2):
        copy = pltpu.make_async_copy(
            inv_h.at[part, :, pl.ds(pl.multiple_of(r * block, 128), block)],
            qmat.at[pl.ds(pl.multiple_of(r * panel, 16), panel), pl.ds(part * block, block)], load_sem.at[n])
        copy.start()
        loads["own"].append(copy)
        n += 1

    def arrive(name):
        for copy in loads[name]:
            copy.wait()

    barrier = pltpu.get_barrier_semaphore()
    for k in range(1, GROUP):
        pl.semaphore_signal(barrier, inc=1, device_id=row_peer(k), device_id_type=MESH)
        pl.semaphore_signal(barrier, inc=1, device_id=col_peer(k), device_id_type=MESH)

    @pl.when(ly > 0)
    def _():
        for k in range(GROUP):
            pl.semaphore_signal(barrier, inc=1, device_id=(ly - 1, k * GROUP + r), device_id_type=MESH)

    @pl.when(ly < depth - 1)
    def _():
        for k in range(GROUP):
            pl.semaphore_signal(barrier, inc=1, device_id=(ly + 1, k * GROUP + r), device_id_type=MESH)

    arrive("leaf")
    arrive("gath")
    first = dot_nt(widen(rs[...]), leaf[...])
    lead[0] = first
    wide = widen(first)
    for j in range(GROUP):
        const[j] = dot_nt(wide, gath[pl.ds(j * block, block), :])

    ends = (ly == 0).astype(jnp.int32) + (ly == depth - 1).astype(jnp.int32)
    pl.semaphore_wait(barrier, 2 * (GROUP - 1) + GROUP * (2 - ends))

    def send_a(s, k):
        pltpu.make_async_remote_copy(
            src_ref=abuf.at[s, lax.rem(r + k, GROUP)], dst_ref=arecv.at[s, k - 1],
            send_sem=send_sem.at[s, 0], recv_sem=recv_sem.at[s, 0],
            device_id=row_peer(k), device_id_type=MESH).start()

    @pl.when(ly == 0)
    def _():
        for j in range(GROUP):
            abuf[0, j] = const[j].astype(BF16)
        for k in ORDER:
            send_a(0, k)

    for k in ORDER:
        to = lax.rem(r + k, GROUP)
        for part in range(2):
            pltpu.make_async_remote_copy(
                src_ref=inv_h.at[part, :, pl.ds(pl.multiple_of(to * block, 128), block)],
                dst_ref=qmat.at[pl.ds(pl.multiple_of(r * panel, 16), panel), pl.ds(part * block, block)],
                send_sem=q_send, recv_sem=q_recv,
                device_id=row_peer(k), device_id_type=MESH).start()

    arrive("below")
    arrive("above")
    leaf_t[...] = leaf[...].T
    leaf_stack = leaf_t[...]
    for coupling, folded, product in ((below, lb_t, xb), (above, la_t, xa)):
        left = expand(coupling[...].T.astype(F32), cells)
        stack = dot_nn(left, leaf_stack)
        folded[...] = stack.astype(BF16)
        left = expand(stack, cells)
        for j in range(GROUP):
            product[:, j * block:(j + 1) * block] = dot_nt(left, gath[pl.ds(j * block, block), :]).astype(BF16)

    arrive("spread")
    for part in range(2):
        for j in range(GROUP):
            turned = pnat[part, :, j * block:(j + 1) * block].T
            per = block // panel
            pt[part, pl.ds(j * per, per)] = turned.reshape(per, panel, cells)

    for slot in range(sep // panel):
        at = slots[slot]
        for part in range(2):
            pts[part, slot * panel:(slot + 1) * panel, :] = pt[part, at]

    def share_spread():
        for k in ORDER:
            to = lax.rem(z + k, GROUP)
            for part in range(2):
                pltpu.make_async_remote_copy(
                    src_ref=pts.at[part, pl.ds(pl.multiple_of(to * block, 128), block)],
                    dst_ref=po.at[pl.ds(part * block, block), pl.ds(pl.multiple_of(z * cells, 128), cells)],
                    send_sem=p_send, recv_sem=p_recv, device_id=col_peer(k), device_id_type=MESH).start()
        for part in range(2):
            po[pl.ds(part * block, block), pl.ds(pl.multiple_of(z * cells, 128), cells)] = (
                pts[part, pl.ds(pl.multiple_of(z * block, 128), block), :])

    p_bytes = po.at[:, pl.ds(0, (GROUP - 1) * cells)]
    q_bytes = qmat.at[pl.ds(0, (GROUP - 1) * panel), :]

    @pl.when(ly >= PLAIN)
    def _():
        share_spread()

    @pl.when(ly > 0)
    def _():
        @pl.when(ly <= PLAIN)
        def _():
            wait_all(fone, one_recv)
            held[0] = fone[...].astype(F32)

        @pl.when(ly > PLAIN)
        def _():
            wait_all(frecv.at[0], y_recv.at[0])
            total = frecv[0, 0].astype(F32)
            for k in range(1, GROUP):
                total = total + frecv[0, k].astype(F32)
            held[0] = total

        wide = widen(held[0])
        for k in ORDER + (0,):
            j = lax.rem(r + k, GROUP)
            cols = pl.ds(pl.multiple_of(j * block, 128), block)
            abuf[0, j] = (const[j] - dot_nn(wide, xa[:, cols])).astype(BF16)
            if k:
                send_a(0, k)
        lead[0] = lead[0] - dot_nn(wide, la_t[...])

    def middle(s):
        wait_all(arecv.at[s], recv_sem.at[s, 0])
        total = abuf[s, r].astype(F32)
        for k in range(GROUP - 1):
            total = total + arecv[s, k].astype(F32)
        bbuf[s] = total.astype(BF16)
        for k in ORDER:
            pltpu.make_async_remote_copy(
                src_ref=bbuf.at[s], dst_ref=brecv.at[s, k - 1],
                send_sem=send_sem.at[s, 1], recv_sem=recv_sem.at[s, 1],
                device_id=col_peer(k), device_id_type=MESH).start()
        if s == 0:
            arrive("own")
            wait_all(q_bytes, q_recv)
            qt[...] = qmat[...].T
        wait_all(brecv.at[s], recv_sem.at[s, 1])
        for k in range(GROUP - 1):
            total = total + brecv[s, k].astype(F32)
        mine = dot_nn(widen(total), qt[...])
        cbuf[s] = mine.astype(BF16)
        for k in ORDER:
            pltpu.make_async_remote_copy(
                src_ref=cbuf.at[s], dst_ref=crecv.at[s, k - 1],
                send_sem=send_sem.at[s, 2], recv_sem=recv_sem.at[s, 2],
                device_id=row_peer(k), device_id_type=MESH).start()
        wait_all(crecv.at[s], recv_sem.at[s, 2])
        for k in range(GROUP - 1):
            mine = mine + crecv[s, k].astype(F32)
        return mine

    def spread_out(s, values, own, sign, to, lane):
        shares = sign * dot_nn(widen(values), po[...])
        for j in range(GROUP):
            prod[j] = shares[:, j * cells:(j + 1) * cells]
            obuf[s, j] = shares[:, j * cells:(j + 1) * cells].astype(BF16)
        total = own + prod[z]
        obuf[s, z] = total.astype(BF16)

        @pl.when(to >= 0)
        def _():
            for k in ORDER + (0,):
                j = lax.rem(z + k, GROUP)
                pltpu.make_async_remote_copy(
                    src_ref=obuf.at[s, j], dst_ref=frecv.at[lane, k],
                    send_sem=y_send.at[s], recv_sem=y_recv.at[lane],
                    device_id=(to, j * GROUP + r), device_id_type=MESH).start()

        for k in ORDER:
            j = lax.rem(z + k, GROUP)
            pltpu.make_async_remote_copy(
                src_ref=obuf.at[s, j], dst_ref=orecv.at[s, k - 1],
                send_sem=o_send.at[s], recv_sem=o_recv.at[s],
                device_id=(ly, j * GROUP + r), device_id_type=MESH).start()
        wait_all(orecv.at[s], o_recv.at[s])
        for k in range(GROUP - 1):
            total = total + orecv[s, k].astype(F32)
        return total

    values = middle(0)
    dbuf[...] = values

    @pl.when(ly < PLAIN)
    def _():
        cbuf[2] = dbuf[...].astype(BF16)
        for k in ORDER:
            pltpu.make_async_remote_copy(
                src_ref=cbuf.at[2], dst_ref=vall.at[z], send_sem=send_sem.at[0, 3], recv_sem=recv_sem.at[0, 3],
                device_id=col_peer(k), device_id_type=MESH).start()
        vall[z] = cbuf[2]
        wait_all(vall.at[pl.ds(0, GROUP - 1)], recv_sem.at[0, 3])
        gathered = jnp.concatenate([vall[k].astype(F32) for k in range(GROUP)], axis=1)
        wide = widen(gathered)
        forward = lead[0] - dot_nn(wide[:, :sep], pts[0]) - dot_nn(wide[:, sep:], pts[1])
        held[1] = forward
        fbuf[...] = forward.astype(BF16)
        pltpu.make_async_remote_copy(
            src_ref=fbuf, dst_ref=fone, send_sem=one_send, recv_sem=one_recv,
            device_id=(ly + 1, me), device_id_type=MESH).start()
        share_spread()

    @pl.when(ly >= PLAIN)
    def _():
        wait_all(p_bytes, p_recv)
        last = ly == depth - 1
        held[1] = spread_out(0, dbuf[...], lead[0], -1.0, jnp.where(last, ly - 1, ly + 1), last.astype(jnp.int32))

    @pl.when(ly == depth - 1)
    def _():
        out[...] = held[1]

    @pl.when(ly < depth - 1)
    def _():
        wait_all(frecv.at[1], y_recv.at[1])
        total = frecv[1, 0].astype(F32)
        for k in range(1, GROUP):
            total = total + frecv[1, k].astype(F32)
        wide = widen(total)
        for k in ORDER + (0,):
            j = lax.rem(r + k, GROUP)
            cols = pl.ds(pl.multiple_of(j * block, 128), block)
            abuf[1, j] = dot_nn(wide, xb[:, cols]).astype(BF16)
            if k:
                send_a(1, k)
        held[1] = held[1] - dot_nn(wide, lb_t[...])
        values = middle(1)

        @pl.when(ly < PLAIN)
        def _():
            wait_all(p_bytes, p_recv)

        out[...] = spread_out(1, values, held[1], 1.0, ly - 1, 1)

    wait_all(q_bytes, q_send)
    wait_all(p_bytes, p_send)

    def sent(s):
        for phase, buf in ((0, arecv), (1, brecv), (2, crecv)):
            wait_all(buf.at[s], send_sem.at[s, phase])

    sent(0)

    @pl.when(ly < PLAIN)
    def _():
        wait_all(vall.at[pl.ds(0, GROUP - 1)], send_sem.at[0, 3])
        wait_all(fone, one_send)

    @pl.when(ly >= PLAIN)
    def _():
        wait_all(frecv.at[0], y_send.at[0])
        wait_all(orecv.at[0], o_send.at[0])

    @pl.when(ly < depth - 1)
    def _():
        sent(1)
        wait_all(orecv.at[1], o_send.at[1])

        @pl.when(ly > 0)
        def _():
            wait_all(frecv.at[1], y_send.at[1])


def local(right_sides, leaf, above, below, gather, inverse, spread, owner):
    depth = lax.axis_size("layer")
    _, _, count, cells = right_sides.shape
    panel, sep = inverse.shape[2], inverse.shape[3]
    block = sep // GROUP
    vmem = pl.BlockSpec(memory_space=pltpu.VMEM)
    hbm = pl.BlockSpec(memory_space=pl.ANY)
    dma = pltpu.SemaphoreType.DMA
    slot = jnp.arange(sep // panel, dtype=jnp.int32)
    slots = jnp.sum(jnp.where(owner[0][:, None] == slot[None, :], slot[:, None], 0), axis=0)
    V = pltpu.VMEM
    out = pl.pallas_call(
        functools.partial(kernel, depth, cells, sep, panel),
        out_shape=jax.ShapeDtypeStruct((ROWS, cells), F32),
        in_specs=[pl.BlockSpec(memory_space=pltpu.SMEM), vmem] + [hbm] * 6,
        out_specs=vmem,
        scratch_shapes=[
            V((cells, 2 * cells), BF16),
            V((cells, 2 * cells), BF16),
            V((cells, 2 * cells), BF16),
            V((sep, 2 * cells), BF16),
            V((block, 2 * block), BF16),
            V((2, cells, sep), BF16),
            V((2 * cells, cells), BF16),
            V((2 * cells, cells), BF16),
            V((2 * cells, cells), BF16),
            V((2 * cells, sep), BF16),
            V((2 * cells, sep), BF16),
            V((2 * block, block), BF16),
            V((2, sep // panel, panel, cells), BF16),
            V((2, sep, cells), BF16),
            V((2 * block, GROUP * cells), BF16),
            V((2, GROUP, ROWS, block), BF16),
            V((2, GROUP - 1, ROWS, block), BF16),
            V((2, ROWS, block), BF16),
            V((2, GROUP - 1, ROWS, block), BF16),
            V((3, ROWS, block), BF16),
            V((2, GROUP - 1, ROWS, block), BF16),
            V((ROWS, block), F32),
            V((GROUP, ROWS, block), BF16),
            V((ROWS, cells), BF16),
            V((ROWS, cells), BF16),
            V((2, GROUP, ROWS, cells), BF16),
            V((2, GROUP - 1, ROWS, cells), BF16),
            V((2, GROUP, ROWS, cells), BF16),
            V((GROUP, ROWS, block), F32),
            V((1, ROWS, cells), F32),
            V((2, ROWS, cells), F32),
            V((GROUP, ROWS, cells), F32),
            dma((11,)),
            dma, dma, dma, dma,
            dma((2, 4)), dma((2, 4)),
            dma, dma,
            dma((2,)), dma((2,)), dma((2,)), dma((2,)),
        ],
        compiler_params=pltpu.CompilerParams(
            collective_id=0, has_side_effects=True, vmem_limit_bytes=60 * 2**20),
        name="sweep",
    )(slots, right_sides.reshape(ROWS, cells), leaf[0], above[0], below[0], gather[0], inverse[0], spread[0])
    return out.reshape(1, 2, count, cells)


def solution(mesh):
    return jax.shard_map(
        local,
        mesh=mesh,
        in_specs=(
            P("layer", None, None, "front"),
            P("layer", None, "front", None),
            P("layer", None, "front", None),
            P("layer", None, "front", None),
            P("layer", None, None, "front"),
            P("layer", None, "front", None),
            P("layer", None, "front", None),
            P("layer", None),
        ),
        out_specs=P("layer", None, None, "front"),
        check_vma=False,
    )
```

time: 2300 us -> 161 us (0.07)
  blocking collectives: 2120 us -> 0 us
  Pallas kernels: 0 us -> 158 us
  matrix products: 87.5 us -> 0 us
  local copies, waits for them, and re-layouts: 46.6 us -> 1.28 us
    psum x7 -> x0, blocking collectives: 1710 us -> none  [layer_solve(): sep_rounded = lax.psum(partial_sums, 'front').astype(jnp.bfloat16)]
    all_gather x7 -> x0, blocking collectives: 412 us -> none  [layer_solve(): stored = lax.all_gather(own_rows, 'front', axis=2, tiled=True)]
    pallas_call x0 -> x1, Pallas kernels: none -> 158 us  [local(): pl.pallas_call(functools.partial(kernel, depth, cells, sep, panel), out_s...]
    dot_general x136 -> x0, matrix products: 87.5 us -> none  [single(): return jnp.dot(right, left.T, preferred_element_type=jnp.float32)]
    reshape x7 -> x0, local copies, waits for them, and re-layouts: 37.8 us -> none  [layer_solve(): panels = stored.reshape(2, count, owner_row.shape[0], own_rows.shape[2])]
  transfers between devices with their start and end apart: 6 -> 0, of which waited for: 6 -> 0; matrix products, arithmetic and copies ran while one was open for 0% -> 0% of each run, Pallas kernels for 0% -> 0%
where the time goes in v2:
time: 161 us
  Pallas kernels  158 us (98%)
    pallas_call x1, Pallas kernels, local(): pl.pallas_call(functools.partial(kernel, depth, cells, sep, panel), out_s...  158 us

profile of v2, /device:TPU:1, one launch (start us, length us, event | category | flops | bytes accessed | tf_op | source)
XLA Modules:
  0.0 160.5 jit_solution(16547200893699173228)
XLA Ops:
  0.0 1.3 select_reduce_fusion.slots
  1.3 158.0 %sweep.1 = f32[8,128]{1,0:T(8,128)} custom-call(s32[64]{0:T(128)} %select_reduce_fusion.slots, f32[8,128]{1,0:T(8,128)} %bitcast.16, bf16[2,128,128]{2,1,0:T(8,128)(2,1)} %bitcast.12, bf16[2,128,128]{2,1,0:T(8,128)(2,1)} %bitcast.13, bf16[2,128,128]{2,1,0:T(8,128)(2,1)} %bitcast.14, bf16[2,5120,128]{2,1,0:T(8,128)(2,1)} %bitcast.9, ...), custom_call_target="tpu_custom_call" | custom-call | tf_op jit(solution)/shard_map/sweep/pallas_call | solution.py:356
  159.3 1.3 copy.10

commit v3 on v2

--- a/solution.py
+++ b/solution.py
@@ -43,9 +43,9 @@
     out,
     leaf, above, below, gath, qmat, pnat, leaf_t, la_t, lb_t, xa, xb, qt, pt, pts, po,
     abuf, arecv, bbuf, brecv, cbuf, crecv, dbuf, vall, fbuf, fone, obuf, orecv, frecv,
-    const, lead, held, prod,
+    const, lead, held, prod, qown, sall, vown,
     load_sem, q_send, q_recv, p_send, p_recv, send_sem, recv_sem, one_send, one_recv,
-    y_send, y_recv, o_send, o_recv,
+    y_send, y_recv, o_send, o_recv, v_send, v_recv,
 ):
     ly = lax.axis_index("layer")
     me = lax.axis_index("front")
@@ -60,6 +60,9 @@
 
     def wait_all(ref, sem):
         pltpu.make_async_copy(ref, ref, sem).wait()
+
+    p_bytes = po.at[:, pl.ds(0, (GROUP - 1) * cells)]
+    q_bytes = qmat.at[pl.ds(0, (GROUP - 1) * panel), :]
 
     loads = {}
     n = 0
@@ -76,10 +79,16 @@
     loads["own"] = []
     for part in range(2):
         copy = pltpu.make_async_copy(
-            inv_h.at[part, :, pl.ds(pl.multiple_of(r * block, 128), block)],
-            qmat.at[pl.ds(pl.multiple_of(r * panel, 16), panel), pl.ds(part * block, block)], load_sem.at[n])
+            inv_h.at[part, :, pl.ds(pl.multiple_of(z * block, 128), block)],
+            qmat.at[pl.ds(pl.multiple_of(z * panel, 16), panel), pl.ds(part * block, block)], load_sem.at[n])
         copy.start()
         loads["own"].append(copy)
+        n += 1
+    loads["panel"] = []
+    for part in range(2):
+        copy = pltpu.make_async_copy(inv_h.at[part], qown.at[:, pl.ds(part * sep, sep)], load_sem.at[n])
+        copy.start()
+        loads["panel"].append(copy)
         n += 1
 
     def arrive(name):
@@ -94,12 +103,12 @@
     @pl.when(ly > 0)
     def _():
         for k in range(GROUP):
-            pl.semaphore_signal(barrier, inc=1, device_id=(ly - 1, k * GROUP + r), device_id_type=MESH)
+            pl.semaphore_signal(barrier, inc=1, device_id=(ly - 1, z * GROUP + k), device_id_type=MESH)
 
     @pl.when(ly < depth - 1)
     def _():
         for k in range(GROUP):
-            pl.semaphore_signal(barrier, inc=1, device_id=(ly + 1, k * GROUP + r), device_id_type=MESH)
+            pl.semaphore_signal(barrier, inc=1, device_id=(ly + 1, z * GROUP + k), device_id_type=MESH)
 
     arrive("leaf")
     arrive("gath")
@@ -112,70 +121,85 @@
     ends = (ly == 0).astype(jnp.int32) + (ly == depth - 1).astype(jnp.int32)
     pl.semaphore_wait(barrier, 2 * (GROUP - 1) + GROUP * (2 - ends))
 
-    def send_a(s, k):
+    def send_a(s, k, at, peer):
         pltpu.make_async_remote_copy(
-            src_ref=abuf.at[s, lax.rem(r + k, GROUP)], dst_ref=arecv.at[s, k - 1],
+            src_ref=abuf.at[s, lax.rem(at + k, GROUP)], dst_ref=arecv.at[s, k - 1],
             send_sem=send_sem.at[s, 0], recv_sem=recv_sem.at[s, 0],
-            device_id=row_peer(k), device_id_type=MESH).start()
+            device_id=peer(k), device_id_type=MESH).start()
 
     @pl.when(ly == 0)
     def _():
         for j in range(GROUP):
             abuf[0, j] = const[j].astype(BF16)
         for k in ORDER:
-            send_a(0, k)
-
-    for k in ORDER:
-        to = lax.rem(r + k, GROUP)
-        for part in range(2):
-            pltpu.make_async_remote_copy(
-                src_ref=inv_h.at[part, :, pl.ds(pl.multiple_of(to * block, 128), block)],
-                dst_ref=qmat.at[pl.ds(pl.multiple_of(r * panel, 16), panel), pl.ds(part * block, block)],
-                send_sem=q_send, recv_sem=q_recv,
-                device_id=row_peer(k), device_id_type=MESH).start()
-
-    arrive("below")
-    arrive("above")
-    leaf_t[...] = leaf[...].T
-    leaf_stack = leaf_t[...]
-    for coupling, folded, product in ((below, lb_t, xb), (above, la_t, xa)):
-        left = expand(coupling[...].T.astype(F32), cells)
-        stack = dot_nn(left, leaf_stack)
-        folded[...] = stack.astype(BF16)
-        left = expand(stack, cells)
-        for j in range(GROUP):
-            product[:, j * block:(j + 1) * block] = dot_nt(left, gath[pl.ds(j * block, block), :]).astype(BF16)
-
-    arrive("spread")
-    for part in range(2):
-        for j in range(GROUP):
-            turned = pnat[part, :, j * block:(j + 1) * block].T
-            per = block // panel
-            pt[part, pl.ds(j * per, per)] = turned.reshape(per, panel, cells)
-
-    for slot in range(sep // panel):
-        at = slots[slot]
-        for part in range(2):
-            pts[part, slot * panel:(slot + 1) * panel, :] = pt[part, at]
-
-    def share_spread():
+            send_a(0, k, r, row_peer)
+
+    def share_inverse():
         for k in ORDER:
             to = lax.rem(z + k, GROUP)
             for part in range(2):
                 pltpu.make_async_remote_copy(
+                    src_ref=inv_h.at[part, :, pl.ds(pl.multiple_of(to * block, 128), block)],
+                    dst_ref=qmat.at[pl.ds(pl.multiple_of(z * panel, 16), panel), pl.ds(part * block, block)],
+                    send_sem=q_send, recv_sem=q_recv,
+                    device_id=col_peer(k), device_id_type=MESH).start()
+
+    def take_inverse():
+        arrive("own")
+        wait_all(q_bytes, q_recv)
+        qt[...] = qmat[...].T
+
+    def fold(pairs):
+        leaf_t[...] = leaf[...].T
+        leaf_stack = leaf_t[...]
+        for coupling, folded, product in pairs:
+            left = expand(coupling[...].T.astype(F32), cells)
+            stack = dot_nn(left, leaf_stack)
+            folded[...] = stack.astype(BF16)
+            left = expand(stack, cells)
+            for j in range(GROUP):
+                product[:, j * block:(j + 1) * block] = dot_nt(left, gath[pl.ds(j * block, block), :]).astype(BF16)
+
+    def turn_spread():
+        for part in range(2):
+            for j in range(GROUP):
+                turned = pnat[part, :, j * block:(j + 1) * block].T
+                per = block // panel
+                pt[part, pl.ds(j * per, per)] = turned.reshape(per, panel, cells)
+        for slot in range(sep // panel):
+            at = slots[slot % GROUP * GROUP + slot // GROUP]
+            for part in range(2):
+                pts[part, slot * panel:(slot + 1) * panel, :] = pt[part, at]
+
+    def share_spread():
+        for k in ORDER:
+            to = lax.rem(r + k, GROUP)
+            for part in range(2):
+                pltpu.make_async_remote_copy(
                     src_ref=pts.at[part, pl.ds(pl.multiple_of(to * block, 128), block)],
-                    dst_ref=po.at[pl.ds(part * block, block), pl.ds(pl.multiple_of(z * cells, 128), cells)],
-                    send_sem=p_send, recv_sem=p_recv, device_id=col_peer(k), device_id_type=MESH).start()
+                    dst_ref=po.at[pl.ds(part * block, block), pl.ds(pl.multiple_of(r * cells, 128), cells)],
+                    send_sem=p_send, recv_sem=p_recv, device_id=row_peer(k), device_id_type=MESH).start()
         for part in range(2):
-            po[pl.ds(part * block, block), pl.ds(pl.multiple_of(z * cells, 128), cells)] = (
-                pts[part, pl.ds(pl.multiple_of(z * block, 128), block), :])
-
-    p_bytes = po.at[:, pl.ds(0, (GROUP - 1) * cells)]
-    q_bytes = qmat.at[pl.ds(0, (GROUP - 1) * panel), :]
+            po[pl.ds(part * block, block), pl.ds(pl.multiple_of(r * cells, 128), cells)] = (
+                pts[part, pl.ds(pl.multiple_of(r * block, 128), block), :])
+
+    arrive("below")
+    arrive("above")
+    arrive("spread")
+
+    @pl.when(ly >= PLAIN)
+    def _():
+        share_inverse()
+
+    turn_spread()
 
     @pl.when(ly >= PLAIN)
     def _():
         share_spread()
+
+    @pl.when(ly > 0)
+    def _():
+        fold(((above, la_t, xa), (below, lb_t, xb)))
 
     @pl.when(ly > 0)
     def _():
@@ -193,17 +217,32 @@
             held[0] = total
 
         wide = widen(held[0])
-        for k in ORDER + (0,):
-            j = lax.rem(r + k, GROUP)
-            cols = pl.ds(pl.multiple_of(j * block, 128), block)
-            abuf[0, j] = (const[j] - dot_nn(wide, xa[:, cols])).astype(BF16)
-            if k:
-                send_a(0, k)
+
+        def send_all(at, peer):
+            for k in ORDER + (0,):
+                j = lax.rem(at + k, GROUP)
+                cols = pl.ds(pl.multiple_of(j * block, 128), block)
+                abuf[0, j] = (const[j] - dot_nn(wide, xa[:, cols])).astype(BF16)
+                if k:
+                    send_a(0, k, at, peer)
+
+        @pl.when(ly < PLAIN)
+        def _():
+            send_all(r, row_peer)
+
+        @pl.when(ly >= PLAIN)
+        def _():
+            send_all(z, col_peer)
+
         lead[0] = lead[0] - dot_nn(wide, la_t[...])
 
-    def middle(s):
+    @pl.when(ly >= PLAIN)
+    def _():
+        take_inverse()
+
+    def sum_block(s, at, peer):
         wait_all(arecv.at[s], recv_sem.at[s, 0])
-        total = abuf[s, r].astype(F32)
+        total = abuf[s, at].astype(F32)
         for k in range(GROUP - 1):
             total = total + arecv[s, k].astype(F32)
         bbuf[s] = total.astype(BF16)
@@ -211,65 +250,93 @@
             pltpu.make_async_remote_copy(
                 src_ref=bbuf.at[s], dst_ref=brecv.at[s, k - 1],
                 send_sem=send_sem.at[s, 1], recv_sem=recv_sem.at[s, 1],
-                device_id=col_peer(k), device_id_type=MESH).start()
-        if s == 0:
-            arrive("own")
-            wait_all(q_bytes, q_recv)
-            qt[...] = qmat[...].T
+                device_id=peer(k), device_id_type=MESH).start()
         wait_all(brecv.at[s], recv_sem.at[s, 1])
         for k in range(GROUP - 1):
             total = total + brecv[s, k].astype(F32)
+        return total
+
+    def value_block(s, total):
         mine = dot_nn(widen(total), qt[...])
         cbuf[s] = mine.astype(BF16)
         for k in ORDER:
             pltpu.make_async_remote_copy(
                 src_ref=cbuf.at[s], dst_ref=crecv.at[s, k - 1],
                 send_sem=send_sem.at[s, 2], recv_sem=recv_sem.at[s, 2],
-                device_id=row_peer(k), device_id_type=MESH).start()
+                device_id=col_peer(k), device_id_type=MESH).start()
         wait_all(crecv.at[s], recv_sem.at[s, 2])
         for k in range(GROUP - 1):
             mine = mine + crecv[s, k].astype(F32)
         return mine
+
+    def panel_block(total):
+        sall[r] = total.astype(BF16)
+        for k in ORDER:
+            pltpu.make_async_remote_copy(
+                src_ref=sall.at[r], dst_ref=sall.at[r], send_sem=send_sem.at[0, 2], recv_sem=recv_sem.at[0, 2],
+                device_id=row_peer(k), device_id_type=MESH).start()
+        wait_all(sall.at[pl.ds(0, GROUP - 1)], recv_sem.at[0, 2])
+        wide = widen(jnp.concatenate([sall[k].astype(F32) for k in range(GROUP)], axis=1))
+        mine = dot_nt(wide, qown[...])
+        vown[z] = jnp.concatenate([mine, jnp.zeros((ROWS, 128 - panel), F32)], axis=1).astype(BF16)
+        for k in ORDER:
+            pltpu.make_async_remote_copy(
+                src_ref=vown.at[z], dst_ref=vown.at[z], send_sem=v_send, recv_sem=v_recv,
+                device_id=col_peer(k), device_id_type=MESH).start()
+        wait_all(vown.at[pl.ds(0, GROUP - 1)], v_recv)
+        return jnp.concatenate([vown[k].astype(F32)[:, :panel] for k in range(GROUP)], axis=1)
 
     def spread_out(s, values, own, sign, to, lane):
         shares = sign * dot_nn(widen(values), po[...])
         for j in range(GROUP):
             prod[j] = shares[:, j * cells:(j + 1) * cells]
             obuf[s, j] = shares[:, j * cells:(j + 1) * cells].astype(BF16)
-        total = own + prod[z]
-        obuf[s, z] = total.astype(BF16)
+        total = own + prod[r]
+        obuf[s, r] = total.astype(BF16)
 
         @pl.when(to >= 0)
         def _():
             for k in ORDER + (0,):
-                j = lax.rem(z + k, GROUP)
+                j = lax.rem(r + k, GROUP)
                 pltpu.make_async_remote_copy(
                     src_ref=obuf.at[s, j], dst_ref=frecv.at[lane, k],
                     send_sem=y_send.at[s], recv_sem=y_recv.at[lane],
-                    device_id=(to, j * GROUP + r), device_id_type=MESH).start()
-
-        for k in ORDER:
-            j = lax.rem(z + k, GROUP)
+                    device_id=(to, z * GROUP + j), device_id_type=MESH).start()
+
+        for k in ORDER:
+            j = lax.rem(r + k, GROUP)
             pltpu.make_async_remote_copy(
                 src_ref=obuf.at[s, j], dst_ref=orecv.at[s, k - 1],
                 send_sem=o_send.at[s], recv_sem=o_recv.at[s],
-                device_id=(ly, j * GROUP + r), device_id_type=MESH).start()
+                device_id=(ly, z * GROUP + j), device_id_type=MESH).start()
         wait_all(orecv.at[s], o_recv.at[s])
         for k in range(GROUP - 1):
             total = total + orecv[s, k].astype(F32)
         return total
 
-    values = middle(0)
-    dbuf[...] = values
+    def second(k):
+        across, along = row_peer(k)[1], col_peer(k)[1]
+        return (ly, jnp.where(ly < PLAIN, along, across))
+
+    sums = sum_block(0, jnp.where(ly < PLAIN, r, z), second)
 
     @pl.when(ly < PLAIN)
     def _():
+        arrive("panel")
+        dbuf[...] = panel_block(sums)
+
+    @pl.when(ly >= PLAIN)
+    def _():
+        dbuf[...] = value_block(0, sums)
+
+    @pl.when(ly < PLAIN)
+    def _():
         cbuf[2] = dbuf[...].astype(BF16)
         for k in ORDER:
             pltpu.make_async_remote_copy(
-                src_ref=cbuf.at[2], dst_ref=vall.at[z], send_sem=send_sem.at[0, 3], recv_sem=recv_sem.at[0, 3],
-                device_id=col_peer(k), device_id_type=MESH).start()
-        vall[z] = cbuf[2]
+                src_ref=cbuf.at[2], dst_ref=vall.at[r], send_sem=send_sem.at[0, 3], recv_sem=recv_sem.at[0, 3],
+                device_id=row_peer(k), device_id_type=MESH).start()
+        vall[r] = cbuf[2]
         wait_all(vall.at[pl.ds(0, GROUP - 1)], recv_sem.at[0, 3])
         gathered = jnp.concatenate([vall[k].astype(F32) for k in range(GROUP)], axis=1)
         wide = widen(gathered)
@@ -279,7 +346,14 @@
         pltpu.make_async_remote_copy(
             src_ref=fbuf, dst_ref=fone, send_sem=one_send, recv_sem=one_recv,
             device_id=(ly + 1, me), device_id_type=MESH).start()
+        share_inverse()
         share_spread()
+
+        @pl.when(ly == 0)
+        def _():
+            fold(((below, lb_t, xb),))
+
+        take_inverse()
 
     @pl.when(ly >= PLAIN)
     def _():
@@ -299,13 +373,13 @@
             total = total + frecv[1, k].astype(F32)
         wide = widen(total)
         for k in ORDER + (0,):
-            j = lax.rem(r + k, GROUP)
+            j = lax.rem(z + k, GROUP)
             cols = pl.ds(pl.multiple_of(j * block, 128), block)
             abuf[1, j] = dot_nn(wide, xb[:, cols]).astype(BF16)
             if k:
-                send_a(1, k)
+                send_a(1, k, z, col_peer)
         held[1] = held[1] - dot_nn(wide, lb_t[...])
-        values = middle(1)
+        values = value_block(1, sum_block(1, z, row_peer))
 
         @pl.when(ly < PLAIN)
         def _():
@@ -321,6 +395,14 @@
             wait_all(buf.at[s], send_sem.at[s, phase])
 
     sent(0)
+
+    @pl.when(ly < PLAIN)
+    def _():
+        wait_all(vown.at[pl.ds(0, GROUP - 1)], v_send)
+
+    @pl.when(ly >= PLAIN)
+    def _():
+        arrive("panel")
 
     @pl.when(ly < PLAIN)
     def _():
@@ -391,11 +473,14 @@
             V((1, ROWS, cells), F32),
             V((2, ROWS, cells), F32),
             V((GROUP, ROWS, cells), F32),
-            dma((11,)),
+            V((panel, 2 * sep), BF16),
+            V((GROUP, ROWS, block), BF16),
+            V((GROUP, ROWS, 128), BF16),
+            dma((13,)),
             dma, dma, dma, dma,
             dma((2, 4)), dma((2, 4)),
             dma, dma,
-            dma((2,)), dma((2,)), dma((2,)), dma((2,)),
+            dma((2,)), dma((2,)), dma((2,)), dma((2,)), dma, dma,
         ],
         compiler_params=pltpu.CompilerParams(
             collective_id=0, has_side_effects=True, vmem_limit_bytes=60 * 2**20),

time: 161 us -> 152 us (0.944)
  Pallas kernels: 158 us -> 150 us
    pallas_call x1, Pallas kernels: 158 us -> 150 us  [local(): pl.pallas_call(functools.partial(kernel, depth, cells, sep, panel), out_s...]
where the time goes in v3:
time: 152 us
  Pallas kernels  150 us (99%)
    pallas_call x1, Pallas kernels, local(): pl.pallas_call(functools.partial(kernel, depth, cells, sep, panel), out_s...  150 us

profile of v3, /device:TPU:1, one launch (start us, length us, event | category | flops | bytes accessed | tf_op | source)
XLA Modules:
  0.0 152.1 jit_solution(12746164692062160300)
XLA Ops:
  0.0 1.3 select_reduce_fusion.slots
  1.3 149.6 %sweep.1 = f32[8,128]{1,0:T(8,128)} custom-call(s32[64]{0:T(128)} %select_reduce_fusion.slots, f32[8,128]{1,0:T(8,128)} %bitcast.16, bf16[2,128,128]{2,1,0:T(8,128)(2,1)} %bitcast.12, bf16[2,128,128]{2,1,0:T(8,128)(2,1)} %bitcast.13, bf16[2,128,128]{2,1,0:T(8,128)(2,1)} %bitcast.14, bf16[2,5120,128]{2,1,0:T(8,128)(2,1)} %bitcast.9, ...), custom_call_target="tpu_custom_call" | custom-call | tf_op jit(solution)/shard_map/sweep/pallas_call | solution.py:438
  150.8 1.3 copy.10

commit v4 on v0

v4 whole, which is shorter than its diff:
```python
import functools

import jax
import jax.numpy as jnp
from jax import lax
from jax.experimental import pallas as pl
from jax.experimental.pallas import tpu as pltpu
from jax.sharding import PartitionSpec as P

MESH = pl.DeviceIdType.MESH
F32 = jnp.float32
BF16 = jnp.bfloat16
ROWS = 8
GROUP = 8
ORDER = (4, 3, 5, 2, 6, 1, 7)


def widen(v):
    turned = pltpu.roll(v, 4, 0)
    row = lax.broadcasted_iota(jnp.int32, v.shape, 0)
    turned = jnp.where(row < 4, -turned, turned)
    return jnp.concatenate([v, turned], axis=1).astype(BF16)


def dot_nt(a, b):
    return lax.dot_general(a, b, (((1,), (1,)), ((), ())), preferred_element_type=F32)


def dot_nn(a, b):
    return lax.dot_general(a, b, (((1,), (0,)), ((), ())), preferred_element_type=F32)


def expand(stack, n):
    top, low = stack[:n], stack[n:]
    return jnp.concatenate(
        [jnp.concatenate([top, -low], axis=1), jnp.concatenate([low, top], axis=1)], axis=0).astype(BF16)


def kernel(
    depth, cells, sep, panel,
    slots, rs, leaf_h, above_h, below_h, gather_h, inv_h, spread_h,
    out,
    leaf, above, below, gath, qmat, pnat, leaf_t, la_t, lb_t, xa, xb, xo, qt, pt, pts, po, qown,
    abuf, arecv, bbuf, brecv, cbuf, crecv, crow, sall, vown, vall, fbuf, fone, obuf, orecv, frecv, frow,
    const, lead, held, prod,
    load_sem, send_sem, recv_sem, bulk_send, bulk_recv, one_send, one_recv,
    y_send, y_recv, w_recv, o_send, o_recv, v_send, v_recv,
):
    ly = lax.axis_index("layer")
    me = lax.axis_index("front")
    z, r = me // GROUP, lax.rem(me, GROUP)
    block = sep // GROUP
    Q_AT, P_AT, X_AT, C_AT = range(4)

    def row_peer(k):
        return (ly, z * GROUP + lax.rem(r + k, GROUP))

    def col_peer(k):
        return (ly, lax.rem(z + k, GROUP) * GROUP + r)

    def wait_all(ref, sem):
        pltpu.make_async_copy(ref, ref, sem).wait()

    def send(src, dst, send_at, recv_at, to):
        pltpu.make_async_remote_copy(
            src_ref=src, dst_ref=dst, send_sem=send_at, recv_sem=recv_at, device_id=to, device_id_type=MESH).start()

    def part_of(index, size):
        return pl.ds(pl.multiple_of(index * size, 128 if size % 128 == 0 else 16), size)

    bulk = (
        qmat.at[pl.ds(0, (GROUP - 1) * panel), :],
        po.at[:, pl.ds(0, (GROUP - 1) * cells)],
        xo.at[pl.ds(0, (GROUP - 1) * 2 * cells), :],
        crow,
    )

    loads = {}
    n = 0
    for name, src, dst in (("leaf", leaf_h, leaf), ("gath", gather_h, gath), ("below", below_h, below), ("above", above_h, above)):
        loads[name] = []
        for part in range(2):
            copy = pltpu.make_async_copy(src.at[part], dst.at[:, pl.ds(part * cells, cells)], load_sem.at[n])
            copy.start()
            loads[name].append(copy)
            n += 1
    loads["spread"] = [pltpu.make_async_copy(spread_h, pnat, load_sem.at[n])]
    loads["spread"][0].start()
    n += 1
    even = lax.rem(ly, 2) == 0
    place = jnp.where(even, z, r)
    loads["own"], loads["panel"] = [], []
    for part in range(2):
        loads["own"].append(pltpu.make_async_copy(
            inv_h.at[part, :, part_of(place, block)],
            qmat.at[part_of(place, panel), pl.ds(part * block, block)], load_sem.at[n]))
        loads["panel"].append(pltpu.make_async_copy(inv_h.at[part], qown.at[:, pl.ds(part * sep, sep)], load_sem.at[n + 1]))
        n += 2
    for copy in loads["own"]:
        copy.start()

    @pl.when(ly == 0)
    def _():
        for copy in loads["panel"]:
            copy.start()

    def arrive(name):
        for copy in loads[name]:
            copy.wait()

    barrier = pltpu.get_barrier_semaphore()

    def greet(to):
        pl.semaphore_signal(barrier, inc=1, device_id=to, device_id_type=MESH)

    for k in range(1, GROUP):
        greet(row_peer(k))
        greet(col_peer(k))
    for low, along_row, along_col in ((0, False, True), (1, True, False), (2, True, True)):
        for mine, other in ((low, low + 1), (low + 1, low)):
            @pl.when(ly == mine)
            def _(other=other, along_row=along_row, along_col=along_col):
                greet((other, me))
                for k in range(1, GROUP):
                    if along_row:
                        greet((other, row_peer(k)[1]))
                    if along_col:
                        greet((other, col_peer(k)[1]))

    arrive("leaf")
    arrive("gath")
    first = dot_nt(widen(rs[...]), leaf[...])
    lead[0] = first
    wide = widen(first)
    for j in range(GROUP):
        const[j] = dot_nt(wide, gath[pl.ds(j * block, block), :])

    greeted = (GROUP, 2 * GROUP, 3 * GROUP - 1, 2 * GROUP - 1)
    extra = jnp.where(ly == 0, greeted[0], jnp.where(ly == 1, greeted[1], jnp.where(ly == 2, greeted[2], greeted[3])))
    pl.semaphore_wait(barrier, 2 * (GROUP - 1) + extra)

    def scatter(s, at, peer, term):
        for k in ORDER + (0,):
            j = lax.rem(at + k, GROUP)
            abuf[s, j] = term(j).astype(BF16)
            if k:
                send(abuf.at[s, j], arecv.at[s, k - 1], send_sem.at[s, 0], recv_sem.at[s, 0], peer(k))

    def scattered(s, at):
        wait_all(arecv.at[s], recv_sem.at[s, 0])
        total = abuf[s, at].astype(F32)
        for k in range(GROUP - 1):
            total = total + arecv[s, k].astype(F32)
        return total

    def add_up(s, phase, mine, buf, recv, peer):
        buf[s] = mine.astype(BF16)
        for k in ORDER:
            send(buf.at[s], recv.at[s, k - 1], send_sem.at[s, phase], recv_sem.at[s, phase], peer(k))
        wait_all(recv.at[s], recv_sem.at[s, phase])
        for k in range(GROUP - 1):
            mine = mine + recv[s, k].astype(F32)
        return mine

    def values_of(s, partial, sums_peer, values_peer):
        sums = add_up(s, 1, partial, bbuf, brecv, sums_peer)
        return add_up(s, 2, dot_nn(widen(sums), qt[...]), cbuf, crecv, values_peer)

    def gather_into(ref, at, peer, send_at, recv_at):
        for k in ORDER:
            send(ref.at[at], ref.at[at], send_at, recv_at, peer(k))
        wait_all(ref.at[pl.ds(0, GROUP - 1)], recv_at)

    def share_inverse(at, peer):
        for k in ORDER:
            for part in range(2):
                send(inv_h.at[part, :, part_of(lax.rem(at + k, GROUP), block)],
                     qmat.at[part_of(at, panel), pl.ds(part * block, block)],
                     bulk_send.at[Q_AT], bulk_recv.at[Q_AT], peer(k))

    def take_inverse():
        arrive("own")
        wait_all(bulk[Q_AT], bulk_recv.at[Q_AT])
        qt[...] = qmat[...].T

    def share_spread(at, peer):
        for k in ORDER:
            for part in range(2):
                send(pts.at[part, part_of(lax.rem(at + k, GROUP), block)],
                     po.at[pl.ds(part * block, block), part_of(at, cells)],
                     bulk_send.at[P_AT], bulk_recv.at[P_AT], peer(k))
        for part in range(2):
            po[pl.ds(part * block, block), part_of(at, cells)] = pts[part, part_of(at, block), :]

    def take_spread():
        wait_all(bulk[P_AT], bulk_recv.at[P_AT])

    def share_product(product):
        for k in ORDER:
            send(product.at[:, part_of(lax.rem(r + k, GROUP), block)], xo.at[part_of(r, 2 * cells), :],
                 bulk_send.at[X_AT], bulk_recv.at[X_AT], row_peer(k))
        xo[part_of(r, 2 * cells), :] = product[:, part_of(r, block)]

    def take_product():
        wait_all(bulk[X_AT], bulk_recv.at[X_AT])

    def fold(pairs):
        leaf_t[...] = leaf[...].T
        leaf_stack = leaf_t[...]
        for coupling, folded, product in pairs:
            left = expand(coupling[...].T.astype(F32), cells)
            stack = dot_nn(left, leaf_stack)
            folded[...] = stack.astype(BF16)
            left = expand(stack, cells)
            for j in range(GROUP):
                product[:, j * block:(j + 1) * block] = dot_nt(left, gath[pl.ds(j * block, block), :]).astype(BF16)

    def turn_spread():
        for part in range(2):
            for j in range(GROUP):
                turned = pnat[part, :, j * block:(j + 1) * block].T
                per = block // panel
                pt[part, pl.ds(j * per, per)] = turned.reshape(per, panel, cells)

    def order_spread(order):
        for place, slot in enumerate(order):
            at = slots[slot]
            for part in range(2):
                pts[part, place * panel:(place + 1) * panel, :] = pt[part, at]

    by_z = range(GROUP * GROUP)
    by_r = [zz * GROUP + rr for rr in range(GROUP) for zz in range(GROUP)]

    def plain_end(values, at, peer):
        vall[at] = values.astype(BF16)
        gather_into(vall, at, peer, send_sem.at[0, 3], recv_sem.at[0, 3])
        wide = widen(jnp.concatenate([vall[k].astype(F32) for k in range(GROUP)], axis=1))
        forward = lead[0] - dot_nn(wide[:, :sep], pts[0]) - dot_nn(wide[:, sep:], pts[1])
        held[...] = forward
        fbuf[...] = forward.astype(BF16)
        send(fbuf, fone, one_send, one_recv, (ly + 1, me))

    def spread_out(s, values, own, sign, at, peer, to, whole):
        shares = sign * dot_nn(widen(values), po[...])
        for j in range(GROUP):
            prod[j] = shares[:, j * cells:(j + 1) * cells]
            obuf[s, j] = shares[:, j * cells:(j + 1) * cells].astype(BF16)
        total = own + prod[at]
        obuf[s, at] = total.astype(BF16)
        if to is not None:
            for k in ORDER + (0,):
                if whole:
                    send(obuf.at[s], frow.at[k], y_send, w_recv, (to, peer(k)[1]))
                else:
                    send(obuf.at[s, lax.rem(at + k, GROUP)], frecv.at[k], y_send, y_recv, (to, peer(k)[1]))
        for k in ORDER:
            send(obuf.at[s, lax.rem(at + k, GROUP)], orecv.at[s, k - 1], o_send.at[s], o_recv.at[s], peer(k))
        wait_all(orecv.at[s], o_recv.at[s])
        for k in range(GROUP - 1):
            total = total + orecv[s, k].astype(F32)
        return total

    def own_cells():
        wait_all(frecv, y_recv)
        total = frecv[0].astype(F32)
        for k in range(1, GROUP):
            total = total + frecv[k].astype(F32)
        return widen(total)

    def row_cells():
        wait_all(frow, w_recv)
        wides = []
        for j in range(GROUP):
            total = frow[0, j].astype(F32)
            for k in range(1, GROUP):
                total = total + frow[k, j].astype(F32)
            prod[j] = total
            wides.append(widen(total))
        return jnp.concatenate(wides, axis=1)

    def columns(product, j):
        return product[:, part_of(j, block)]

    arrive_maps = ("below", "above", "spread")

    @pl.when(ly == 0)
    def _():
        scatter(0, r, row_peer, lambda j: const[j])
        for name in arrive_maps:
            arrive(name)
        turn_spread()
        order_spread(by_r)
        sums = add_up(0, 1, scattered(0, r), bbuf, brecv, col_peer)
        sall[r] = sums.astype(BF16)
        gather_into(sall, r, row_peer, send_sem.at[0, 2], recv_sem.at[0, 2])
        arrive("panel")
        wide = widen(jnp.concatenate([sall[k].astype(F32) for k in range(GROUP)], axis=1))
        mine = dot_nt(wide, qown[...])
        vown[z] = jnp.concatenate([mine, jnp.zeros((ROWS, 128 - panel), F32)], axis=1).astype(BF16)
        gather_into(vown, z, col_peer, v_send, v_recv)
        values = jnp.concatenate([vown[k].astype(F32)[:, :panel] for k in range(GROUP)], axis=1)
        plain_end(values, r, row_peer)
        share_inverse(z, col_peer)
        share_spread(r, row_peer)
        fold(((below, lb_t, xb),))
        take_inverse()
        take_spread()

    @pl.when(ly == 1)
    def _():
        share_inverse(r, row_peer)
        for name in arrive_maps:
            arrive(name)
        fold(((above, la_t, xa), (below, lb_t, xb)))
        turn_spread()
        order_spread(by_z)
        take_inverse()
        wait_all(fone, one_recv)
        wide = widen(fone[...].astype(F32))
        scatter(0, r, row_peer, lambda j: const[j] - dot_nn(wide, columns(xa, j)))
        lead[0] = lead[0] - dot_nn(wide, la_t[...])
        plain_end(values_of(0, scattered(0, r), col_peer, row_peer), z, col_peer)
        share_product(xb)
        share_spread(z, col_peer)
        take_product()
        wide = row_cells()
        partial = dot_nn(wide, xo[...])
        held[...] = held[...] - dot_nn(widen(prod[r]), lb_t[...])
        values = values_of(1, partial, col_peer, row_peer)
        take_spread()
        out[...] = spread_out(1, values, held[...], 1.0, z, col_peer, 0, False)

    @pl.when(ly == 2)
    def _():
        share_inverse(z, col_peer)
        for name in arrive_maps:
            arrive(name)
        turn_spread()
        order_spread(by_r)
        share_spread(r, row_peer)
        fold(((above, la_t, xa), (below, lb_t, xb)))
        take_inverse()
        take_spread()
        wait_all(fone, one_recv)
        wide = widen(fone[...].astype(F32))
        scatter(0, z, col_peer, lambda j: const[j] - dot_nn(wide, columns(xa, j)))
        lead[0] = lead[0] - dot_nn(wide, la_t[...])
        values = values_of(0, scattered(0, z), row_peer, col_peer)
        held[...] = spread_out(0, values, lead[0], -1.0, r, row_peer, 3, True)
        wait_all(frow, y_send)

    @pl.when(ly == 3)
    def _():
        share_inverse(r, row_peer)
        for k in ORDER:
            send(const.at[lax.rem(r + k, GROUP)], crow.at[k - 1], bulk_send.at[C_AT], bulk_recv.at[C_AT], row_peer(k))
        for name in arrive_maps:
            arrive(name)
        turn_spread()
        order_spread(by_z)
        share_spread(z, col_peer)
        fold(((above, la_t, xa),))
        share_product(xa)
        wait_all(bulk[C_AT], bulk_recv.at[C_AT])
        known = const[r]
        for k in range(GROUP - 1):
            known = known + crow[k]
        crow[0] = known
        take_inverse()
        take_product()
        wide = row_cells()
        partial = crow[0] - dot_nn(wide, xo[...])
        lead[0] = lead[0] - dot_nn(widen(prod[r]), la_t[...])
        values = values_of(0, partial, col_peer, row_peer)
        take_spread()
        out[...] = spread_out(0, values, lead[0], -1.0, z, col_peer, 2, False)

    @pl.when(even)
    def _():
        wide = own_cells()
        scatter(1, z, col_peer, lambda j: dot_nn(wide, columns(xb, j)))
        held[...] = held[...] - dot_nn(wide, lb_t[...])
        values = values_of(1, scattered(1, z), row_peer, col_peer)

        @pl.when(ly == 2)
        def _():
            out[...] = spread_out(1, values, held[...], 1.0, r, row_peer, 1, True)
            wait_all(frow, y_send)

        @pl.when(ly == 0)
        def _():
            out[...] = spread_out(1, values, held[...], 1.0, r, row_peer, None, False)

    wait_all(bulk[Q_AT], bulk_send.at[Q_AT])
    wait_all(bulk[P_AT], bulk_send.at[P_AT])

    def left(s, phases):
        for phase in phases:
            wait_all((arecv, brecv, crecv)[phase].at[s], send_sem.at[s, phase])

    @pl.when(ly == 0)
    def _():
        left(0, (0, 1, 2))
        wait_all(vown.at[pl.ds(0, GROUP - 1)], v_send)
        left(1, (0, 1, 2))
        wait_all(orecv.at[1], o_send.at[1])

    @pl.when(ly == 1)
    def _():
        left(0, (0, 1, 2))
        left(1, (1, 2))
        wait_all(bulk[X_AT], bulk_send.at[X_AT])
        wait_all(frecv, y_send)
        wait_all(orecv.at[1], o_send.at[1])

    @pl.when(ly < 2)
    def _():
        wait_all(vall.at[pl.ds(0, GROUP - 1)], send_sem.at[0, 3])
        wait_all(fone, one_send)

    @pl.when(ly == 2)
    def _():
        left(0, (0, 1, 2))
        left(1, (0, 1, 2))
        for s in range(2):
            wait_all(orecv.at[s], o_send.at[s])

    @pl.when(ly == 3)
    def _():
        left(0, (1, 2))
        wait_all(bulk[X_AT], bulk_send.at[X_AT])
        wait_all(bulk[C_AT], bulk_send.at[C_AT])
        wait_all(frecv, y_send)
        wait_all(orecv.at[0], o_send.at[0])


def local(right_sides, leaf, above, below, gather, inverse, spread, owner):
    depth = lax.axis_size("layer")
    _, _, count, cells = right_sides.shape
    panel, sep = inverse.shape[2], inverse.shape[3]
    block = sep // GROUP
    vmem = pl.BlockSpec(memory_space=pltpu.VMEM)
    hbm = pl.BlockSpec(memory_space=pl.ANY)
    dma = pltpu.SemaphoreType.DMA
    slot = jnp.arange(sep // panel, dtype=jnp.int32)
    slots = jnp.sum(jnp.where(owner[0][:, None] == slot[None, :], slot[:, None], 0), axis=0)
    V = pltpu.VMEM
    out = pl.pallas_call(
        functools.partial(kernel, depth, cells, sep, panel),
        out_shape=jax.ShapeDtypeStruct((ROWS, cells), F32),
        in_specs=[pl.BlockSpec(memory_space=pltpu.SMEM), vmem] + [hbm] * 6,
        out_specs=vmem,
        scratch_shapes=[
            V((cells, 2 * cells), BF16),
            V((cells, 2 * cells), BF16),
            V((cells, 2 * cells), BF16),
            V((sep, 2 * cells), BF16),
            V((block, 2 * block), BF16),
            V((2, cells, sep), BF16),
            V((2 * cells, cells), BF16),
            V((2 * cells, cells), BF16),
            V((2 * cells, cells), BF16),
            V((2 * cells, sep), BF16),
            V((2 * cells, sep), BF16),
            V((GROUP * 2 * cells, block), BF16),
            V((2 * block, block), BF16),
            V((2, sep // panel, panel, cells), BF16),
            V((2, sep, cells), BF16),
            V((2 * block, GROUP * cells), BF16),
            V((panel, 2 * sep), BF16),
            V((2, GROUP, ROWS, block), BF16),
            V((2, GROUP - 1, ROWS, block), BF16),
            V((2, ROWS, block), BF16),
            V((2, GROUP - 1, ROWS, block), BF16),
            V((2, ROWS, block), BF16),
            V((2, GROUP - 1, ROWS, block), BF16),
            V((GROUP - 1, ROWS, block), F32),
            V((GROUP, ROWS, block), BF16),
            V((GROUP, ROWS, 128), BF16),
            V((GROUP, ROWS, block), BF16),
            V((ROWS, cells), BF16),
            V((ROWS, cells), BF16),
            V((2, GROUP, ROWS, cells), BF16),
            V((2, GROUP - 1, ROWS, cells), BF16),
            V((GROUP, ROWS, cells), BF16),
            V((GROUP, GROUP, ROWS, cells), BF16),
            V((GROUP, ROWS, block), F32),
            V((1, ROWS, cells), F32),
            V((ROWS, cells), F32),
            V((GROUP, ROWS, cells), F32),
            dma((13,)),
            dma((2, 4)), dma((2, 4)),
            dma((4,)), dma((4,)),
            dma, dma,
            dma, dma, dma,
            dma((2,)), dma((2,)),
            dma, dma,
        ],
        compiler_params=pltpu.CompilerParams(
            collective_id=0, has_side_effects=True, vmem_limit_bytes=60 * 2**20),
        name="sweep",
    )(slots, right_sides.reshape(ROWS, cells), leaf[0], above[0], below[0], gather[0], inverse[0], spread[0])
    return out.reshape(1, 2, count, cells)


def solution(mesh):
    return jax.shard_map(
        local,
        mesh=mesh,
        in_specs=(
            P("layer", None, None, "front"),
            P("layer", None, "front", None),
            P("layer", None, "front", None),
            P("layer", None, "front", None),
            P("layer", None, None, "front"),
            P("layer", None, "front", None),
            P("layer", None, "front", None),
            P("layer", None),
        ),
        out_specs=P("layer", None, None, "front"),
        check_vma=False,
    )
```

time: 2300 us -> 144 us (0.06)
  blocking collectives: 2120 us -> 0 us
  Pallas kernels: 0 us -> 141 us
  matrix products: 87.5 us -> 0 us
  local copies, waits for them, and re-layouts: 46.6 us -> 1.28 us
    psum x7 -> x0, blocking collectives: 1710 us -> none  [layer_solve(): sep_rounded = lax.psum(partial_sums, 'front').astype(jnp.bfloat16)]
    all_gather x7 -> x0, blocking collectives: 412 us -> none  [layer_solve(): stored = lax.all_gather(own_rows, 'front', axis=2, tiled=True)]
    pallas_call x0 -> x1, Pallas kernels: none -> 141 us  [local(): pl.pallas_call(functools.partial(kernel, depth, cells, sep, panel), out_s...]
    dot_general x136 -> x0, matrix products: 87.5 us -> none  [single(): return jnp.dot(right, left.T, preferred_element_type=jnp.float32)]
    reshape x7 -> x0, local copies, waits for them, and re-layouts: 37.8 us -> none  [layer_solve(): panels = stored.reshape(2, count, owner_row.shape[0], own_rows.shape[2])]
  transfers between devices with their start and end apart: 6 -> 0, of which waited for: 6 -> 0; matrix products, arithmetic and copies ran while one was open for 0% -> 0% of each run, Pallas kernels for 0% -> 0%
where the time goes in v4:
time: 144 us
  Pallas kernels  141 us (98%)
    pallas_call x1, Pallas kernels, local(): pl.pallas_call(functools.partial(kernel, depth, cells, sep, panel), out_s...  141 us

profile of v4, /device:TPU:1, one launch (start us, length us, event | category | flops | bytes accessed | tf_op | source)
XLA Modules:
  0.0 144.0 jit_solution(1444994145163972520)
XLA Ops:
  0.0 1.3 select_reduce_fusion.slots
  1.3 141.5 %sweep.1 = f32[8,128]{1,0:T(8,128)} custom-call(s32[64]{0:T(128)} %select_reduce_fusion.slots, f32[8,128]{1,0:T(8,128)} %bitcast.16, bf16[2,128,128]{2,1,0:T(8,128)(2,1)} %bitcast.12, bf16[2,128,128]{2,1,0:T(8,128)(2,1)} %bitcast.13, bf16[2,128,128]{2,1,0:T(8,128)(2,1)} %bitcast.14, bf16[2,5120,128]{2,1,0:T(8,128)(2,1)} %bitcast.9, ...), custom_call_target="tpu_custom_call" | custom-call | tf_op jit(solution)/shard_map/sweep/pallas_call | solution.py:448
  142.7 1.3 copy.10

commit v5 on v4

--- a/solution.py
+++ b/solution.py
@@ -162,13 +162,17 @@
             mine = mine + recv[s, k].astype(F32)
         return mine
 
-    def values_of(s, partial, sums_peer, values_peer):
+    def values_of(s, partial, sums_peer, values_peer, late=False):
         sums = add_up(s, 1, partial, bbuf, brecv, sums_peer)
+        if late:
+            take_inverse()
         return add_up(s, 2, dot_nn(widen(sums), qt[...]), cbuf, crecv, values_peer)
 
-    def gather_into(ref, at, peer, send_at, recv_at):
+    def gather_into(ref, at, peer, send_at, recv_at, meanwhile=None):
         for k in ORDER:
             send(ref.at[at], ref.at[at], send_at, recv_at, peer(k))
+        if meanwhile:
+            meanwhile()
         wait_all(ref.at[pl.ds(0, GROUP - 1)], recv_at)
 
     def share_inverse(at, peer):
@@ -195,11 +199,11 @@
     def take_spread():
         wait_all(bulk[P_AT], bulk_recv.at[P_AT])
 
-    def share_product(product):
+    def share_product(product, at, peer):
         for k in ORDER:
-            send(product.at[:, part_of(lax.rem(r + k, GROUP), block)], xo.at[part_of(r, 2 * cells), :],
-                 bulk_send.at[X_AT], bulk_recv.at[X_AT], row_peer(k))
-        xo[part_of(r, 2 * cells), :] = product[:, part_of(r, block)]
+            send(product.at[:, part_of(lax.rem(at + k, GROUP), block)], xo.at[part_of(at, 2 * cells), :],
+                 bulk_send.at[X_AT], bulk_recv.at[X_AT], peer(k))
+        xo[part_of(at, 2 * cells), :] = product[:, part_of(at, block)]
 
     def take_product():
         wait_all(bulk[X_AT], bulk_recv.at[X_AT])
@@ -241,20 +245,34 @@
         send(fbuf, fone, one_send, one_recv, (ly + 1, me))
 
     def spread_out(s, values, own, sign, at, peer, to, whole):
-        shares = sign * dot_nn(widen(values), po[...])
-        for j in range(GROUP):
-            prod[j] = shares[:, j * cells:(j + 1) * cells]
-            obuf[s, j] = shares[:, j * cells:(j + 1) * cells].astype(BF16)
-        total = own + prod[at]
-        obuf[s, at] = total.astype(BF16)
-        if to is not None:
+        wide = widen(values)
+
+        def pass_on(k):
+            j = lax.rem(at + k, GROUP)
+            if to is not None and not whole:
+                send(obuf.at[s, j], frecv.at[k], y_send, y_recv, (to, peer(k)[1]))
+            if k:
+                send(obuf.at[s, j], orecv.at[s, k - 1], o_send.at[s], o_recv.at[s], peer(k))
+
+        if whole:
+            shares = sign * dot_nn(wide, po[...])
+            for j in range(GROUP):
+                prod[j] = shares[:, j * cells:(j + 1) * cells]
+                obuf[s, j] = shares[:, j * cells:(j + 1) * cells].astype(BF16)
+            total = own + prod[at]
+            obuf[s, at] = total.astype(BF16)
             for k in ORDER + (0,):
-                if whole:
-                    send(obuf.at[s], frow.at[k], y_send, w_recv, (to, peer(k)[1]))
-                else:
-                    send(obuf.at[s, lax.rem(at + k, GROUP)], frecv.at[k], y_send, y_recv, (to, peer(k)[1]))
-        for k in ORDER:
-            send(obuf.at[s, lax.rem(at + k, GROUP)], orecv.at[s, k - 1], o_send.at[s], o_recv.at[s], peer(k))
+                send(obuf.at[s], frow.at[k], y_send, w_recv, (to, peer(k)[1]))
+            for k in ORDER:
+                pass_on(k)
+        else:
+            for k in ORDER + (0,):
+                j = lax.rem(at + k, GROUP)
+                share = sign * dot_nn(wide, po[:, part_of(j, cells)])
+                if not k:
+                    share = total = own + share
+                obuf[s, j] = share.astype(BF16)
+                pass_on(k)
         wait_all(orecv.at[s], o_recv.at[s])
         for k in range(GROUP - 1):
             total = total + orecv[s, k].astype(F32)
@@ -267,7 +285,7 @@
             total = total + frecv[k].astype(F32)
         return widen(total)
 
-    def row_cells():
+    def group_cells():
         wait_all(frow, w_recv)
         wides = []
         for j in range(GROUP):
@@ -297,14 +315,19 @@
         wide = widen(jnp.concatenate([sall[k].astype(F32) for k in range(GROUP)], axis=1))
         mine = dot_nt(wide, qown[...])
         vown[z] = jnp.concatenate([mine, jnp.zeros((ROWS, 128 - panel), F32)], axis=1).astype(BF16)
-        gather_into(vown, z, col_peer, v_send, v_recv)
+        gather_into(vown, z, col_peer, v_send, v_recv, lambda: fold(((below, lb_t, xb),)))
+        share_product(xb, z, col_peer)
+        share_inverse(z, col_peer)
         values = jnp.concatenate([vown[k].astype(F32)[:, :panel] for k in range(GROUP)], axis=1)
         plain_end(values, r, row_peer)
-        share_inverse(z, col_peer)
         share_spread(r, row_peer)
-        fold(((below, lb_t, xb),))
-        take_inverse()
         take_spread()
+        take_product()
+        wide = group_cells()
+        partial = dot_nn(wide, xo[...])
+        held[...] = held[...] - dot_nn(widen(prod[z]), lb_t[...])
+        values = values_of(1, partial, row_peer, col_peer, True)
+        out[...] = spread_out(1, values, held[...], 1.0, r, row_peer, None, False)
 
     @pl.when(ly == 1)
     def _():
@@ -320,15 +343,15 @@
         scatter(0, r, row_peer, lambda j: const[j] - dot_nn(wide, columns(xa, j)))
         lead[0] = lead[0] - dot_nn(wide, la_t[...])
         plain_end(values_of(0, scattered(0, r), col_peer, row_peer), z, col_peer)
-        share_product(xb)
+        share_product(xb, r, row_peer)
         share_spread(z, col_peer)
         take_product()
-        wide = row_cells()
+        wide = group_cells()
         partial = dot_nn(wide, xo[...])
         held[...] = held[...] - dot_nn(widen(prod[r]), lb_t[...])
         values = values_of(1, partial, col_peer, row_peer)
         take_spread()
-        out[...] = spread_out(1, values, held[...], 1.0, z, col_peer, 0, False)
+        out[...] = spread_out(1, values, held[...], 1.0, z, col_peer, 0, True)
 
     @pl.when(ly == 2)
     def _():
@@ -348,6 +371,12 @@
         values = values_of(0, scattered(0, z), row_peer, col_peer)
         held[...] = spread_out(0, values, lead[0], -1.0, r, row_peer, 3, True)
         wait_all(frow, y_send)
+        wide = own_cells()
+        scatter(1, z, col_peer, lambda j: dot_nn(wide, columns(xb, j)))
+        held[...] = held[...] - dot_nn(wide, lb_t[...])
+        values = values_of(1, scattered(1, z), row_peer, col_peer)
+        out[...] = spread_out(1, values, held[...], 1.0, r, row_peer, 1, True)
+        wait_all(frow, y_send)
 
     @pl.when(ly == 3)
     def _():
@@ -360,7 +389,7 @@
         order_spread(by_z)
         share_spread(z, col_peer)
         fold(((above, la_t, xa),))
-        share_product(xa)
+        share_product(xa, r, row_peer)
         wait_all(bulk[C_AT], bulk_recv.at[C_AT])
         known = const[r]
         for k in range(GROUP - 1):
@@ -368,29 +397,13 @@
         crow[0] = known
         take_inverse()
         take_product()
-        wide = row_cells()
+        wide = group_cells()
         partial = crow[0] - dot_nn(wide, xo[...])
         lead[0] = lead[0] - dot_nn(widen(prod[r]), la_t[...])
         values = values_of(0, partial, col_peer, row_peer)
         take_spread()
         out[...] = spread_out(0, values, lead[0], -1.0, z, col_peer, 2, False)
 
-    @pl.when(even)
-    def _():
-        wide = own_cells()
-        scatter(1, z, col_peer, lambda j: dot_nn(wide, columns(xb, j)))
-        held[...] = held[...] - dot_nn(wide, lb_t[...])
-        values = values_of(1, scattered(1, z), row_peer, col_peer)
-
-        @pl.when(ly == 2)
-        def _():
-            out[...] = spread_out(1, values, held[...], 1.0, r, row_peer, 1, True)
-            wait_all(frow, y_send)
-
-        @pl.when(ly == 0)
-        def _():
-            out[...] = spread_out(1, values, held[...], 1.0, r, row_peer, None, False)
-
     wait_all(bulk[Q_AT], bulk_send.at[Q_AT])
     wait_all(bulk[P_AT], bulk_send.at[P_AT])
 
@@ -402,7 +415,8 @@
     def _():
         left(0, (0, 1, 2))
         wait_all(vown.at[pl.ds(0, GROUP - 1)], v_send)
-        left(1, (0, 1, 2))
+        wait_all(bulk[X_AT], bulk_send.at[X_AT])
+        left(1, (1, 2))
         wait_all(orecv.at[1], o_send.at[1])
 
     @pl.when(ly == 1)
@@ -410,7 +424,7 @@
         left(0, (0, 1, 2))
         left(1, (1, 2))
         wait_all(bulk[X_AT], bulk_send.at[X_AT])
-        wait_all(frecv, y_send)
+        wait_all(frow, y_send)
         wait_all(orecv.at[1], o_send.at[1])
 
     @pl.when(ly < 2)

time: 144 us -> 141 us (0.979)
  Pallas kernels: 141 us -> 138 us
    pallas_call x1, Pallas kernels: 141 us -> 138 us  [local(): pl.pallas_call(functools.partial(kernel, depth, cells, sep, panel), out_s...]
where the time goes in v5:
time: 141 us
  Pallas kernels  138 us (98%)
    pallas_call x1, Pallas kernels, local(): pl.pallas_call(functools.partial(kernel, depth, cells, sep, panel), out_s...  138 us

profile of v5, /device:TPU:1, one launch (start us, length us, event | category | flops | bytes accessed | tf_op | source)
XLA Modules:
  0.0 140.6 jit_solution(2008968290081121971)
XLA Ops:
  0.0 1.3 select_reduce_fusion.slots
  1.3 138.1 %sweep.1 = f32[8,128]{1,0:T(8,128)} custom-call(s32[64]{0:T(128)} %select_reduce_fusion.slots, f32[8,128]{1,0:T(8,128)} %bitcast.16, bf16[2,128,128]{2,1,0:T(8,128)(2,1)} %bitcast.12, bf16[2,128,128]{2,1,0:T(8,128)(2,1)} %bitcast.13, bf16[2,128,128]{2,1,0:T(8,128)(2,1)} %bitcast.14, bf16[2,5120,128]{2,1,0:T(8,128)(2,1)} %bitcast.9, ...), custom_call_target="tpu_custom_call" | custom-call | tf_op jit(solution)/shard_map/sweep/pallas_call | solution.py:462
  139.3 1.3 copy.10

commit v6 on v5

--- a/solution.py
+++ b/solution.py
@@ -38,11 +38,11 @@
 
 def kernel(
     depth, cells, sep, panel,
-    slots, rs, leaf_h, above_h, below_h, gather_h, inv_h, spread_h,
+    owner, rs, leaf_h, above_h, below_h, gather_h, inv_h, spread_h,
     out,
     leaf, above, below, gath, qmat, pnat, leaf_t, la_t, lb_t, xa, xb, xo, qt, pt, pts, po, qown,
     abuf, arecv, bbuf, brecv, cbuf, crecv, crow, sall, vown, vall, fbuf, fone, obuf, orecv, frecv, frow,
-    const, lead, held, prod,
+    const, lead, held, prod, table, slots,
     load_sem, send_sem, recv_sem, bulk_send, bulk_recv, one_send, one_recv,
     y_send, y_recv, w_recv, o_send, o_recv, v_send, v_recv,
 ):
@@ -127,6 +127,17 @@
                     if along_col:
                         greet((other, col_peer(k)[1]))
 
+    count = sep // panel
+    table[...] = jnp.full((1, 128), count, jnp.int32)
+    table[:, :count] = owner[...]
+    stored_in = jnp.broadcast_to(table[...], (128, 128)).T
+    panel_at = lax.broadcasted_iota(jnp.int32, (128, 128), 0)
+    slot_at = lax.broadcasted_iota(jnp.int32, (128, 128), 1)
+    hit = (stored_in == slot_at) & (panel_at < count)
+    table[...] = jnp.max(jnp.where(hit, panel_at, 0), axis=0, keepdims=True)
+    loads["slots"] = [pltpu.make_async_copy(table, slots, load_sem.at[n])]
+    loads["slots"][0].start()
+
     arrive("leaf")
     arrive("gath")
     first = dot_nt(widen(rs[...]), leaf[...])
@@ -227,8 +238,9 @@
                 pt[part, pl.ds(j * per, per)] = turned.reshape(per, panel, cells)
 
     def order_spread(order):
+        arrive("slots")
         for place, slot in enumerate(order):
-            at = slots[slot]
+            at = slots[0, slot]
             for part in range(2):
                 pts[part, place * panel:(place + 1) * panel, :] = pt[part, at]
 
@@ -456,13 +468,11 @@
     vmem = pl.BlockSpec(memory_space=pltpu.VMEM)
     hbm = pl.BlockSpec(memory_space=pl.ANY)
     dma = pltpu.SemaphoreType.DMA
-    slot = jnp.arange(sep // panel, dtype=jnp.int32)
-    slots = jnp.sum(jnp.where(owner[0][:, None] == slot[None, :], slot[:, None], 0), axis=0)
     V = pltpu.VMEM
     out = pl.pallas_call(
         functools.partial(kernel, depth, cells, sep, panel),
-        out_shape=jax.ShapeDtypeStruct((ROWS, cells), F32),
-        in_specs=[pl.BlockSpec(memory_space=pltpu.SMEM), vmem] + [hbm] * 6,
+        out_shape=pltpu.VMEM((ROWS, cells), F32),
+        in_specs=[vmem, vmem] + [hbm] * 6,
         out_specs=vmem,
         scratch_shapes=[
             V((cells, 2 * cells), BF16),
@@ -502,7 +512,9 @@
             V((1, ROWS, cells), F32),
             V((ROWS, cells), F32),
             V((GROUP, ROWS, cells), F32),
-            dma((13,)),
+            V((1, 128), jnp.int32),
+            pltpu.SMEM((1, 128), jnp.int32),
+            dma((14,)),
             dma((2, 4)), dma((2, 4)),
             dma((4,)), dma((4,)),
             dma, dma,
@@ -513,7 +525,7 @@
         compiler_params=pltpu.CompilerParams(
             collective_id=0, has_side_effects=True, vmem_limit_bytes=60 * 2**20),
         name="sweep",
-    )(slots, right_sides.reshape(ROWS, cells), leaf[0], above[0], below[0], gather[0], inverse[0], spread[0])
+    )(owner, right_sides.reshape(ROWS, cells), leaf[0], above[0], below[0], gather[0], inverse[0], spread[0])
     return out.reshape(1, 2, count, cells)
 
 

time: 141 us -> 138 us (0.979)
  no operation moved by 1% of the time
where the time goes in v6:
time: 138 us
  Pallas kernels  138 us (100%)
    pallas_call x1, Pallas kernels, local(): pl.pallas_call(functools.partial(kernel, depth, cells, sep, panel), out_s...  138 us

profile of v6, /device:TPU:1, one launch (start us, length us, event | category | flops | bytes accessed | tf_op | source)
XLA Modules:
  0.0 138.1 jit_solution(4316832021912795120)
XLA Ops:
  0.0 137.5 %sweep.1 = f32[8,128]{1,0:T(8,128)S(1)} custom-call(s32[1,64]{1,0:T(1,128)} %owner.1, f32[8,128]{1,0:T(8,128)} %bitcast.15, bf16[2,128,128]{2,1,0:T(8,128)(2,1)} %bitcast.12, bf16[2,128,128]{2,1,0:T(8,128)(2,1)} %bitcast.13, bf16[2,128,128]{2,1,0:T(8,128)(2,1)} %bitcast.14, bf16[2,5120,128]{2,1,0:T(8,128)(2,1)} %bitcast.9, bf16[2,80,5120]{2,1,0:T(8,128)(2,1)} %bitcast.11, ...), custom_call_target="tpu_custom_call" | custom-call | tf_op jit(solution)/shard_map/sweep/pallas_call | solution.py:472
  137.5 0.6 copy.10

commit v7 on v6

--- a/solution.py
+++ b/solution.py
@@ -267,14 +267,16 @@
                 send(obuf.at[s, j], orecv.at[s, k - 1], o_send.at[s], o_recv.at[s], peer(k))
 
         if whole:
-            shares = sign * dot_nn(wide, po[...])
-            for j in range(GROUP):
-                prod[j] = shares[:, j * cells:(j + 1) * cells]
-                obuf[s, j] = shares[:, j * cells:(j + 1) * cells].astype(BF16)
+            half = GROUP // 2
+            for low in (0, half):
+                shares = sign * dot_nn(wide, po[:, low * cells:(low + half) * cells])
+                for i in range(half):
+                    share = shares[:, i * cells:(i + 1) * cells]
+                    prod[low + i] = share
+                    obuf[s, low + i] = jnp.where(at == low + i, share + own, share).astype(BF16)
+                for k in ORDER + (0,):
+                    send(obuf.at[s, pl.ds(low, half)], frow.at[k, pl.ds(low, half)], y_send, w_recv, (to, peer(k)[1]))
             total = own + prod[at]
-            obuf[s, at] = total.astype(BF16)
-            for k in ORDER + (0,):
-                send(obuf.at[s], frow.at[k], y_send, w_recv, (to, peer(k)[1]))
             for k in ORDER:
                 pass_on(k)
         else:

time: 138 us -> 139 us (level)
  no operation moved by 1% of the time
where the time goes in v7:
time: 139 us
  Pallas kernels  138 us (99%)
    pallas_call x1, Pallas kernels, local(): pl.pallas_call(functools.partial(kernel, depth, cells, sep, panel), out_s...  138 us

profile of v7, /device:TPU:1, one launch (start us, length us, event | category | flops | bytes accessed | tf_op | source)
XLA Modules:
  0.0 138.5 jit_solution(10001197110081368180)
XLA Ops:
  0.0 137.9 %sweep.1 = f32[8,128]{1,0:T(8,128)S(1)} custom-call(s32[1,64]{1,0:T(1,128)} %owner.1, f32[8,128]{1,0:T(8,128)} %bitcast.15, bf16[2,128,128]{2,1,0:T(8,128)(2,1)} %bitcast.12, bf16[2,128,128]{2,1,0:T(8,128)(2,1)} %bitcast.13, bf16[2,128,128]{2,1,0:T(8,128)(2,1)} %bitcast.14, bf16[2,5120,128]{2,1,0:T(8,128)(2,1)} %bitcast.9, bf16[2,80,5120]{2,1,0:T(8,128)(2,1)} %bitcast.11, ...), custom_call_target="tpu_custom_call" | custom-call | tf_op jit(solution)/shard_map/sweep/pallas_call | solution.py:474
  137.9 0.6 copy.10

commit v8 on v6

--- a/solution.py
+++ b/solution.py
@@ -40,7 +40,7 @@
     depth, cells, sep, panel,
     owner, rs, leaf_h, above_h, below_h, gather_h, inv_h, spread_h,
     out,
-    leaf, above, below, gath, qmat, pnat, leaf_t, la_t, lb_t, xa, xb, xo, qt, pt, pts, po, qown,
+    leaf, above, below, gath, qmat, pnat, leaf_t, la_t, lb_t, xa, xb, xo, qt, pt, pts, po, qown, qown_t,
     abuf, arecv, bbuf, brecv, cbuf, crecv, crow, sall, vown, vall, fbuf, fone, obuf, orecv, frecv, frow,
     const, lead, held, prod, table, slots,
     load_sem, send_sem, recv_sem, bulk_send, bulk_recv, one_send, one_recv,
@@ -320,12 +320,14 @@
             arrive(name)
         turn_spread()
         order_spread(by_r)
+        arrive("panel")
+        for j in range(2 * GROUP):
+            qown_t[j * block:(j + 1) * block, :] = qown[:, j * block:(j + 1) * block].T
         sums = add_up(0, 1, scattered(0, r), bbuf, brecv, col_peer)
         sall[r] = sums.astype(BF16)
         gather_into(sall, r, row_peer, send_sem.at[0, 2], recv_sem.at[0, 2])
-        arrive("panel")
         wide = widen(jnp.concatenate([sall[k].astype(F32) for k in range(GROUP)], axis=1))
-        mine = dot_nt(wide, qown[...])
+        mine = dot_nn(wide, qown_t[...])
         vown[z] = jnp.concatenate([mine, jnp.zeros((ROWS, 128 - panel), F32)], axis=1).astype(BF16)
         gather_into(vown, z, col_peer, v_send, v_recv, lambda: fold(((below, lb_t, xb),)))
         share_product(xb, z, col_peer)
@@ -492,6 +494,7 @@
             V((2, sep, cells), BF16),
             V((2 * block, GROUP * cells), BF16),
             V((panel, 2 * sep), BF16),
+            V((2 * sep, panel), BF16),
             V((2, GROUP, ROWS, block), BF16),
             V((2, GROUP - 1, ROWS, block), BF16),
             V((2, ROWS, block), BF16),

time: 138 us -> 138 us (level)
  no operation moved by 1% of the time
where the time goes in v8:
time: 138 us
  Pallas kernels  137 us (99%)
    pallas_call x1, Pallas kernels, local(): pl.pallas_call(functools.partial(kernel, depth, cells, sep, panel), out_s...  137 us

profile of v8, /device:TPU:1, one launch (start us, length us, event | category | flops | bytes accessed | tf_op | source)
XLA Modules:
  0.0 137.6 jit_solution(18300844930039834874)
XLA Ops:
  0.0 137.0 %sweep.1 = f32[8,128]{1,0:T(8,128)S(1)} custom-call(s32[1,64]{1,0:T(1,128)} %owner.1, f32[8,128]{1,0:T(8,128)} %bitcast.15, bf16[2,128,128]{2,1,0:T(8,128)(2,1)} %bitcast.12, bf16[2,128,128]{2,1,0:T(8,128)(2,1)} %bitcast.13, bf16[2,128,128]{2,1,0:T(8,128)(2,1)} %bitcast.14, bf16[2,5120,128]{2,1,0:T(8,128)(2,1)} %bitcast.9, bf16[2,80,5120]{2,1,0:T(8,128)(2,1)} %bitcast.11, ...), custom_call_target="tpu_custom_call" | custom-call | tf_op jit(solution)/shard_map/sweep/pallas_call | solution.py:474
  137.0 0.6 copy.10
